TPU v7x, 32 devices: a whole 2x2x4 slice. The times are simulated.
32 devices in a mesh: dp: 16 (over z, y, core), tensor: 2 (over x).
Axes of the slice: x: 2, y: 2, z: 4, core: 2. Of those that a mesh axis runs over, the one named last changes fastest.
Arguments:
- tokens: bfloat16 [64, 256, 1152], P(('dp', 'tensor')), may hold values from -6 to 6
- condition: bfloat16 [64, 1152], P('dp', 'tensor'), may hold values from -6 to 6
- keep_count: int32 [64], P('dp'), may hold values from 64 to 192, as said below
- token_order: int32 [64, 256], P(('dp', 'tensor')), may hold values from 0 to 255, each once within a row
- w_ada: bfloat16 [1152, 6912], P('tensor'), may hold values from -0.1875 to 0.1875
- b_ada: bfloat16 [6912], replicated, may hold values from -3 to 3
- w_qkv: bfloat16 [1152, 3, 1152], P(None, None, 'tensor'), may hold values from -0.1875 to 0.1875
- b_qv: bfloat16 [2, 1152], P(None, 'tensor'), may hold values from -3 to 3
- w_proj: bfloat16 [1152, 1152], P('tensor'), may hold values from -0.5 to 0.5
- b_proj: bfloat16 [1152], replicated, may hold values from -2 to 2
- w_up: bfloat16 [1152, 4608], P(None, 'tensor'), may hold values from -0.1875 to 0.1875
- b_up: bfloat16 [4608], P('tensor'), may hold values from -3 to 3
- w_down: bfloat16 [4608, 1152], P('tensor'), may hold values from -0.09375 to 0.09375
- b_down: bfloat16 [1152], replicated, may hold values from -2 to 2
- cotangent: bfloat16 [64, 256, 1152], P(('dp', 'tensor')), may hold values from -6 to 6
Outputs:
- block_out: bfloat16 [64, 256, 1152], P(('dp', 'tensor'))
- grad_tokens: float32 [64, 256, 1152], P(('dp', 'tensor'))
- grad_condition: float32 [64, 1152], P('dp', 'tensor')
- grad_w_ada: float32 [1152, 6912], P('tensor')
- grad_b_ada: float32 [6912], replicated
- grad_w_qkv: float32 [1152, 3, 1152], P(None, None, 'tensor')
- grad_b_qv: float32 [2, 1152], P(None, 'tensor')
- grad_w_proj: float32 [1152, 1152], P('tensor')
- grad_b_proj: float32 [1152], replicated
- grad_w_up: float32 [1152, 4608], P(None, 'tensor')
- grad_b_up: float32 [4608], P('tensor')
- grad_w_down: float32 [4608, 1152], P('tensor')
- grad_b_down: float32 [1152], replicated
Inputs may be any that keep to these rules, and one draw needn't show every extreme that they name: Image i keeps the tokens at token_order[i, 0] to token_order[i, keep_count[i] - 1]; in every draw some image keeps 192. `token_order`: each row is a permutation of 0 to 255.
All inputs are finite; a program needn't handle non-finite values.
Results may differ from a plain program's by a relative error of at most 0.022.
The roundings to bfloat16 on the way count: a program that leaves them out, or rounds other values in their place, can miss the bound.
Values may be sent and summed in bfloat16 or wider, within the bound.
No kernel may reach another device: no remote copies, remote signals or barrier semaphores. Data moves between devices by JAX's collectives and lax.ppermute only.
A program may use at most 192 MiB of HBM per device.

v0:
```python
import jax
import jax.numpy as jnp
from jax import lax
from jax.sharding import PartitionSpec as P

HD = 72


NORM_EPS = 1e-06
MASKED = -1e30
GELU_C = 0.7978845608028654
GELU_A = 0.044715


def gelu_tanh(values):
    return 0.5 * values * (1.0 + jnp.tanh(GELU_C * (values + GELU_A * values * values * values)))


def gelu_slope(values):
    tanh_part = jnp.tanh(GELU_C * (values + GELU_A * values * values * values))
    return 0.5 * (1.0 + tanh_part) + 0.5 * values * (1.0 - tanh_part * tanh_part) * GELU_C * (
        1.0 + 3.0 * GELU_A * values * values
    )


def norm_rows(values):
    centre = values - jnp.mean(values, axis=-1, keepdims=True)
    inv_std = lax.rsqrt(jnp.mean(centre * centre, axis=-1, keepdims=True) + NORM_EPS)
    return (centre * inv_std, inv_std)


def norm_back(grad_norm, normed, inv_std):
    return inv_std * (
        grad_norm
        - jnp.mean(grad_norm, axis=-1, keepdims=True)
        - normed * jnp.mean(grad_norm * normed, axis=-1, keepdims=True)
    )


def matmul_nn(left_mat, right_mat):
    return jnp.dot(left_mat, right_mat, preferred_element_type=jnp.float32)


def matmul_tn(left_mat, right_mat):
    return lax.dot_general(
        left_mat, right_mat, (((0,), (0,)), ((), ())), preferred_element_type=jnp.float32
    )


def matmul_nt(left_mat, right_mat):
    return lax.dot_general(
        left_mat, right_mat, (((1,), (1,)), ((), ())), preferred_element_type=jnp.float32
    )


def scores_of(queries, key_rows, key_live, attn_scale):
    scores = (
        jnp.einsum("bqhe,bkhe->bhqk", queries, key_rows, preferred_element_type=jnp.float32)
        * attn_scale
    )
    return jnp.where(key_live[:, None, None, :], scores, MASKED)


def attend(queries, key_rows, value_rows, key_live, attn_scale):
    scores = scores_of(queries, key_rows, key_live, attn_scale)
    row_top = jnp.max(scores, axis=-1, keepdims=True)
    exp_scores = jnp.exp(scores - row_top)
    totals = jnp.sum(exp_scores, axis=-1, keepdims=True)
    prob_rows = (exp_scores / totals).astype(jnp.bfloat16)
    attended = jnp.einsum(
        "bhqk,bkhe->bqhe", prob_rows, value_rows, preferred_element_type=jnp.float32
    ).astype(jnp.bfloat16)
    return (attended, row_top + jnp.log(totals))


def attend_back(queries, key_rows, value_rows, key_live, attn_scale, log_total, grad_att):
    scores = scores_of(queries, key_rows, key_live, attn_scale)
    probs_full = jnp.exp(scores - log_total)
    grad_value = jnp.einsum(
        "bhqk,bqhe->bkhe",
        probs_full.astype(jnp.bfloat16),
        grad_att,
        preferred_element_type=jnp.float32,
    )
    grad_probs = jnp.einsum(
        "bqhe,bkhe->bhqk", grad_att, value_rows, preferred_element_type=jnp.float32
    )
    inner_sum = jnp.sum(probs_full * grad_probs, axis=-1, keepdims=True)
    grad_scores = (probs_full * (grad_probs - inner_sum)).astype(jnp.bfloat16)
    grad_query = (
        jnp.einsum("bhqk,bkhe->bqhe", grad_scores, key_rows, preferred_element_type=jnp.float32)
        * attn_scale
    )
    grad_key = (
        jnp.einsum("bhqk,bqhe->bkhe", grad_scores, queries, preferred_element_type=jnp.float32)
        * attn_scale
    )
    return (grad_query, grad_key, grad_value)


def body(
    tokens,
    condition,
    keep_count,
    token_order,
    w_ada,
    b_ada,
    w_qkv,
    b_qv,
    w_proj,
    b_proj,
    w_up,
    b_up,
    w_down,
    b_down,
    cotangent,
):
    own_images, seq_len, feat_width = tokens.shape
    group_images = keep_count.shape[0]
    keep_most = 3 * seq_len // 4
    attn_scale = HD ** (-0.5)
    flat_rows = own_images * keep_most
    own_start = lax.axis_index("tensor") * own_images
    own_counts = lax.dynamic_slice_in_dim(keep_count, own_start, own_images)
    slot_ids = jnp.arange(keep_most, dtype=jnp.int32)
    own_live = slot_ids[None, :] < own_counts[:, None]
    group_live = slot_ids[None, :] < keep_count[:, None]
    slot_place = token_order[:, :keep_most]
    picked = jnp.take_along_axis(tokens, slot_place[:, :, None], axis=1)
    x_rows = jnp.where(own_live[:, :, None], picked.astype(jnp.float32), 0.0)
    positions = jnp.arange(seq_len, dtype=jnp.int32)
    rank_of = jnp.sum(
        jnp.where(token_order[:, :, None] == positions[None, None, :], positions[None, :, None], 0),
        axis=1,
    )
    kept_pos = rank_of < own_counts[:, None]
    rank_slot = jnp.minimum(rank_of, keep_most - 1)
    silu_in = condition.astype(jnp.float32)
    silu_cond = jax.nn.silu(silu_in).astype(jnp.bfloat16)
    mod_own = lax.psum_scatter(
        matmul_nn(silu_cond, w_ada), "tensor", scatter_dimension=0, tiled=True
    ) + b_ada.astype(jnp.float32)
    mod_blocks = [
        mod_own[:, column_block * feat_width : (column_block + 1) * feat_width][:, None, :]
        for column_block in range(6)
    ]
    shift_one, scale_one, gate_one, shift_two, scale_two, gate_two = mod_blocks
    normed_one, inv_one = norm_rows(x_rows)
    mod_in_one = (
        (normed_one * (1.0 + scale_one) + shift_one)
        .astype(jnp.bfloat16)
        .reshape(flat_rows, feat_width)
    )
    in_one_all = lax.all_gather(mod_in_one, "tensor", axis=0, tiled=True)
    head_cols = w_qkv.shape[2]
    head_count = head_cols // HD
    qkv_weight = w_qkv.reshape(feat_width, 3 * head_cols)
    qkv_all = matmul_nn(in_one_all, qkv_weight).reshape(group_images, keep_most, 3, head_count, HD)
    qv_bias = b_qv.astype(jnp.float32).reshape(2, head_count, HD)
    queries = (qkv_all[:, :, 0] + qv_bias[0]).astype(jnp.bfloat16)
    key_rows = qkv_all[:, :, 1].astype(jnp.bfloat16)
    value_rows = (qkv_all[:, :, 2] + qv_bias[1]).astype(jnp.bfloat16)
    attended, log_total = attend(queries, key_rows, value_rows, group_live, attn_scale)
    att_flat = attended.reshape(group_images * keep_most, head_cols)
    proj_sum = lax.psum_scatter(
        matmul_nn(att_flat, w_proj).astype(jnp.bfloat16), "tensor", scatter_dimension=0, tiled=True
    ).astype(jnp.float32)
    branch_one = (proj_sum + b_proj.astype(jnp.float32)).reshape(own_images, keep_most, feat_width)
    resid_one = x_rows + gate_one * branch_one
    normed_two, inv_two = norm_rows(resid_one)
    mod_in_two = (
        (normed_two * (1.0 + scale_two) + shift_two)
        .astype(jnp.bfloat16)
        .reshape(flat_rows, feat_width)
    )
    in_two_all = lax.all_gather(mod_in_two, "tensor", axis=0, tiled=True)
    pre_act = matmul_nn(in_two_all, w_up) + b_up.astype(jnp.float32)
    hidden = gelu_tanh(pre_act).astype(jnp.bfloat16)
    branch_two = lax.psum_scatter(
        matmul_nn(hidden, w_down).astype(jnp.bfloat16), "tensor", scatter_dimension=0, tiled=True
    ).astype(jnp.float32)
    branch_two = (branch_two + b_down.astype(jnp.float32)).reshape(
        own_images, keep_most, feat_width
    )
    resid_two = resid_one + gate_two * branch_two
    out_rows = jnp.take_along_axis(resid_two, rank_slot[:, :, None], axis=1)
    block_out = jnp.where(kept_pos[:, :, None], out_rows, tokens.astype(jnp.float32)).astype(
        jnp.bfloat16
    )
    grad_picked = jnp.take_along_axis(cotangent, slot_place[:, :, None], axis=1)
    grad_two = jnp.where(own_live[:, :, None], grad_picked.astype(jnp.float32), 0.0)
    grad_gate_two = jnp.sum(grad_two * branch_two, axis=1)
    grad_branch_two = (gate_two * grad_two).astype(jnp.bfloat16).reshape(flat_rows, feat_width)
    branch_grads_all = lax.all_gather(grad_branch_two, "tensor", axis=0, tiled=True)
    grad_b_down = jnp.sum(branch_grads_all, axis=0, dtype=jnp.float32)
    grad_w_down = matmul_tn(hidden, branch_grads_all)
    grad_pre = (matmul_nt(branch_grads_all, w_down) * gelu_slope(pre_act)).astype(jnp.bfloat16)
    grad_b_up = jnp.sum(grad_pre, axis=0, dtype=jnp.float32)
    grad_w_up = matmul_tn(in_two_all, grad_pre)
    grad_in_two = lax.psum_scatter(
        matmul_nt(grad_pre, w_up).astype(jnp.bfloat16), "tensor", scatter_dimension=0, tiled=True
    ).astype(jnp.float32)
    grad_in_two = grad_in_two.reshape(own_images, keep_most, feat_width)
    grad_shift_two = jnp.sum(grad_in_two, axis=1)
    grad_scale_two = jnp.sum(grad_in_two * normed_two, axis=1)
    grad_one = grad_two + norm_back(grad_in_two * (1.0 + scale_two), normed_two, inv_two)
    grad_gate_one = jnp.sum(grad_one * branch_one, axis=1)
    grad_branch_one = (gate_one * grad_one).astype(jnp.bfloat16).reshape(flat_rows, feat_width)
    branch_one_all = lax.all_gather(grad_branch_one, "tensor", axis=0, tiled=True)
    grad_b_proj = jnp.sum(branch_one_all, axis=0, dtype=jnp.float32)
    grad_w_proj = matmul_tn(att_flat, branch_one_all)
    grad_att = (
        matmul_nt(branch_one_all, w_proj)
        .astype(jnp.bfloat16)
        .reshape(group_images, keep_most, head_count, HD)
    )
    grad_query, grad_key, grad_value = attend_back(
        queries, key_rows, value_rows, group_live, attn_scale, log_total, grad_att
    )
    grad_qkv = jnp.stack([grad_query, grad_key, grad_value], axis=2).astype(jnp.bfloat16)
    grad_b_qv = jnp.stack(
        [
            jnp.sum(grad_qkv[:, :, 0], axis=(0, 1), dtype=jnp.float32).reshape(head_cols),
            jnp.sum(grad_qkv[:, :, 2], axis=(0, 1), dtype=jnp.float32).reshape(head_cols),
        ]
    )
    grad_qkv_flat = grad_qkv.reshape(group_images * keep_most, 3 * head_cols)
    grad_w_qkv = matmul_tn(in_one_all, grad_qkv_flat).reshape(feat_width, 3, head_cols)
    grad_in_one = lax.psum_scatter(
        matmul_nt(grad_qkv_flat, qkv_weight).astype(jnp.bfloat16),
        "tensor",
        scatter_dimension=0,
        tiled=True,
    ).astype(jnp.float32)
    grad_in_one = grad_in_one.reshape(own_images, keep_most, feat_width)
    grad_shift_one = jnp.sum(grad_in_one, axis=1)
    grad_scale_one = jnp.sum(grad_in_one * normed_one, axis=1)
    grad_rows = grad_one + norm_back(grad_in_one * (1.0 + scale_one), normed_one, inv_one)
    grad_placed = jnp.take_along_axis(grad_rows, rank_slot[:, :, None], axis=1)
    grad_tokens = jnp.where(kept_pos[:, :, None], grad_placed, cotangent.astype(jnp.float32))
    grad_mod_own = jnp.concatenate(
        [
            grad_shift_one,
            grad_scale_one,
            grad_gate_one,
            grad_shift_two,
            grad_scale_two,
            grad_gate_two,
        ],
        axis=1,
    ).astype(jnp.bfloat16)
    grad_mod_all = lax.all_gather(grad_mod_own, "tensor", axis=0, tiled=True)
    grad_w_ada = matmul_tn(silu_cond, grad_mod_all)
    grad_b_ada = jnp.sum(grad_mod_all, axis=0, dtype=jnp.float32)
    sigmoid_c = jax.nn.sigmoid(silu_in)
    grad_condition = matmul_nt(grad_mod_all, w_ada) * (
        sigmoid_c * (1.0 + silu_in * (1.0 - sigmoid_c))
    )
    summed = (
        lax.psum(grad_w_ada.astype(jnp.bfloat16), "dp").astype(jnp.float32),
        lax.psum(grad_b_ada.astype(jnp.bfloat16), "dp").astype(jnp.float32),
        lax.psum(grad_w_qkv.astype(jnp.bfloat16), "dp").astype(jnp.float32),
        lax.psum(grad_b_qv.astype(jnp.bfloat16), "dp").astype(jnp.float32),
        lax.psum(grad_w_proj.astype(jnp.bfloat16), "dp").astype(jnp.float32),
        lax.psum(grad_b_proj.astype(jnp.bfloat16), "dp").astype(jnp.float32),
        lax.psum(grad_w_up.astype(jnp.bfloat16), "dp").astype(jnp.float32),
        lax.psum(grad_b_up.astype(jnp.bfloat16), "dp").astype(jnp.float32),
        lax.psum(grad_w_down.astype(jnp.bfloat16), "dp").astype(jnp.float32),
        lax.psum(grad_b_down.astype(jnp.bfloat16), "dp").astype(jnp.float32),
    )
    return (
        block_out,
        grad_tokens,
        grad_condition,
        summed[0],
        summed[1],
        summed[2],
        summed[3],
        summed[4],
        summed[5],
        summed[6],
        summed[7],
        summed[8],
        summed[9],
    )


def solution(mesh):
    placed = (
        P(("dp", "tensor"), None, None),
        P("dp", "tensor"),
        P("dp"),
        P(("dp", "tensor"), None),
        P("tensor", None),
        P(),
        P(None, None, "tensor"),
        P(None, "tensor"),
        P("tensor", None),
        P(),
        P(None, "tensor"),
        P("tensor"),
        P("tensor", None),
        P(),
        P(("dp", "tensor"), None, None),
    )
    return jax.shard_map(
        body,
        mesh=mesh,
        in_specs=placed,
        out_specs=(
            P(("dp", "tensor"), None, None),
            P(("dp", "tensor"), None, None),
            P("dp", "tensor"),
            P("tensor", None),
            P(),
            P(None, None, "tensor"),
            P(None, "tensor"),
            P("tensor", None),
            P(),
            P(None, "tensor"),
            P("tensor"),
            P("tensor", None),
            P(),
        ),
        check_vma=False,
    )
```

profile of v0, /device:TPU:0, one launch (start us, length us, event | category | flops | bytes accessed | tf_op | source)
XLA Modules:
  0.0 815.6 jit_solution(16835164611115682654)
XLA Ops:
  7.3 5.2 fusion.46
  12.9 5.7 gather_fusion
  20.9 15.8 %all-reduce.6.cloned.1.call-done = f32[4,6912]{1,0:T(4,128)} async-done(((f32[4,6912]{1,0:T(4,128)}), f32[4,6912]{1,0:T(4,128)}) %all-reduce.6.cloned.1.call-update) | async-done | bytes 110608
  38.3 2.2 add_convert_fusion.1
  41.0 29.1 %all-gather.6.cloned.1.call-done = bf16[768,1152]{1,0:T(8,128)(2,1)} async-done(((bf16[384,1152]{1,0:T(8,128)(2,1)}), bf16[768,1152]{1,0:T(8,128)(2,1)}) %all-gather.6.cloned.1.call-update) | async-done | bytes 1769488 | tf_op jit(solution)/shard_map/all_gather | solution.py:154
  70.1 7.2 fusion.52
  77.3 1.7 fusion.50
  79.1 1.1 fusion.7
  80.3 2.1 copy-done.2
  82.3 1.5 fusion.28
  85.9 2.9 convolution_convert_fusion.5
  90.0 7.0 gather_fusion.2
  97.1 20.2 %reduce-scatter.5.cloned.1.call-done = bf16[384,1152]{1,0:T(8,128)(2,1)} async-done(((bf16[768,1152]{1,0:T(8,128)(2,1)}), bf16[384,1152]{1,0:T(8,128)(2,1)}) %reduce-scatter.5.cloned.1.call-update) | async-done | bytes 884752 | tf_op jit(solution)/shard_map/reduce_scatter | solution.py:165
  117.3 1.4 convert_add_fusion.1
  119.0 2.0 fusion.48
  121.3 1.3 add_convert_fusion
  123.3 28.9 %all-gather.8.cloned.1.call-done = bf16[768,1152]{1,0:T(8,128)(2,1)} async-done(((bf16[384,1152]{1,0:T(8,128)(2,1)}), bf16[768,1152]{1,0:T(8,128)(2,1)}) %all-gather.8.cloned.1.call-update) | async-done | bytes 1769488 | tf_op jit(solution)/shard_map/all_gather | solution.py:176
  152.1 10.7 %fusion.53 = f32[768,2304]{1,0:T(8,128)} fusion(bf16[768,1152]{1,0:T(8,128)(2,1)} %all-gather.8.cloned.1.call-done, bf16[1152,2304]{1,0:T(8,128)(2,1)} %param.29), kind=kOutput, calls=%fused_computation.136 | convolution fusion | flops 4076863488 | bytes 14155776 | tf_op jit(solution)/shard_map/dot_general | solution.py:41
  162.9 20.7 %all-gather.10.cloned.1.call-done = bf16[768,1152]{1,0:T(8,128)(2,1)} async-done(((bf16[384,1152]{1,0:T(8,128)(2,1)}), bf16[768,1152]{1,0:T(8,128)(2,1)}) %all-gather.10.cloned.1.call-update) | async-done | bytes 1769488 | tf_op jit(solution)/shard_map/all_gather | solution.py:194
  183.5 11.6 %fusion.51 = (bf16[2304]{0:T(1024)(128)(2,1)}, bf16[768,2304]{1,0:T(8,128)(2,1)S(1)}) fusion(f32[768,2304]{1,0:T(8,128)} %fusion.53, f32[2304]{0:T(1024)S(1)} %convert_element_type.199, bf16[768,1152]{1,0:T(8,128)(2,1)} %all-gather.10.cloned.1.call-done, bf16[2304,1152]{1,0:T(8,128)(2,1)} %param.31), kind=kOutput, calls=%fused_computation.134 | convolution fusion | flops 4114020096 | bytes 17708544 | tf_op jit(solution)/shard_map/dot_general | solution.py:51
  195.2 1.8 copy-done.59
  196.9 8.4 %convolution_convert_fusion.6 = bf16[768,1152]{1,0:T(8,128)(2,1)} fusion(bf16[768,2304]{1,0:T(8,128)(2,1)S(1)} %get-tuple-element.54, bf16[1152,2304]{1,0:T(8,128)(2,1)} %param.29), kind=kOutput, calls=%fused_computation.29 | convolution fusion | flops 4077748224 | bytes 10616832 | tf_op jit(solution)/shard_map/dot_general | solution.py:51
  205.4 28.4 %reduce-scatter.9.cloned.1.call-done = bf16[384,1152]{1,0:T(8,128)(2,1)} async-done(((bf16[768,1152]{1,0:T(8,128)(2,1)}), bf16[384,1152]{1,0:T(8,128)(2,1)}) %reduce-scatter.9.cloned.1.call-update) | async-done | bytes 884752 | tf_op jit(solution)/shard_map/reduce_scatter | solution.py:200
  233.9 1.4 fusion.20
  235.4 2.6 multiply_reduce_fusion.2
  238.0 2.5 multiply_reduce_fusion.3
  240.6 2.5 multiply_convert_fusion.2
  243.4 12.0 %convolution_convert_fusion.7 = bf16[768,1152]{1,0:T(8,128)(2,1)} fusion(bf16[2304,1152]{1,0:T(8,128)(2,1)} %param.31, f32[768,2304]{1,0:T(8,128)} %fusion.53, f32[2304]{0:T(1024)S(1)} %convert_element_type.199), kind=kOutput, calls=%fused_computation.30 | convolution fusion | flops 4095442944 | bytes 14164992 | tf_op jit(solution)/shard_map/dot_general | solution.py:41
  255.5 17.2 %all-gather.12.cloned.1.call-done = bf16[768,1152]{1,0:T(8,128)(2,1)} async-done(((bf16[384,1152]{1,0:T(8,128)(2,1)}), bf16[768,1152]{1,0:T(8,128)(2,1)}) %all-gather.12.cloned.1.call-update) | async-done | bytes 1769488 | tf_op jit(solution)/shard_map/all_gather | solution.py:209
  272.6 3.7 convolution_convert_fusion.9
  276.4 3.0 reshape.236
  279.4 6.3 multiply_reduce_fusion
  285.7 1.8 multiply_convert_fusion.1
  287.5 2.4 multiply_bitcast_fusion.1
  289.9 2.8 multiply_bitcast_fusion
  292.7 1.1 fusion.24
  294.7 1.8 copy-done.13
  296.5 4.5 copy.57
  301.0 7.4 convert_element_type.216
  308.4 7.9 convolution_convert_fusion.4
  316.4 9.4 %convolution_convert_fusion.1 = bf16[1152,2304]{1,0:T(8,128)(2,1)} fusion(bf16[768,1152]{1,0:T(8,128)(2,1)} %all-gather.8.cloned.1.call-done, bf16[768,2304]{1,0:T(8,128)(2,1)} %copy-done.59), kind=kOutput, calls=%fused_computation.5 | convolution fusion | flops 4079517696 | bytes 10616832 | tf_op jit(solution)/shard_map/dot_general | solution.py:45
  325.8 13.3 %convolution_convert_fusion = bf16[2304,1152]{1,0:T(8,128)(2,1)} fusion(bf16[768,1152]{1,0:T(8,128)(2,1)S(1)} %copy-done.24, f32[768,2304]{1,0:T(8,128)} %fusion.53, f32[2304]{0:T(1024)S(1)} %copy-done.48), kind=kOutput, calls=%fused_computation.4 | convolution fusion | flops 4097212416 | bytes 14164992 | tf_op jit(solution)/shard_map/dot_general | solution.py:45
  339.1 1.4 convert_add_fusion
  341.2 2.4 convolution_convert_fusion.8
  344.6 5.2 convolution_convert_fusion.3
  349.8 3.4 multiply_reduce_fusion.4
  353.3 4.5 all-gather
  357.9 5.6 convolution_convert_fusion.2
  364.4 1.9 reduce_sum.241
  366.4 1.7 multiply_add_fusion.3
  368.0 8.6 %gather_fusion.1 = bf16[512,1152]{1,0:T(8,128)(2,1)} fusion(bf16[2,192,1152]{2,1,0:T(8,128)(2,1)S(1)} %multiply_add_fusion.3, s32[512]{0:T(512)S(1)} %bitcast.141), kind=kCustom, calls=%fused_computation.1.clone | custom fusion | bytes 2363392 | tf_op jit(solution)/shard_map/jit(take_along_axis)/gather | solution.py:186
  376.6 2.9 fusion.17
  380.2 1.8 reduce_sum.239
  382.5 63.3 %all-reduce.1 = (bf16[6912]{0:T(1024)(128)(2,1)S(1)}, bf16[2,576]{1,0:T(2,128)(2,1)S(1)}, bf16[1152]{0:T(1024)(128)(2,1)S(1)}, bf16[2304]{0:T(1024)(128)(2,1)S(1)}, bf16[1152]{0:T(1024)(128)(2,1)S(1)}) all-reduce(bf16[6912]{0:T(1024)(128)(2,1)S(1)} %reduce_sum.236, ...), channel_id=1, replica_groups=mesh['dp'=16,'tensor'=2] {'dp'}, use_global_device_ids=true, to_apply=%region_25.28 | all-reduce | flops 12672 | bytes 50688 | tf_op jit(solution)/shard_map/psum | solution.py:261
  448.8 2.5 multiply_add_fusion.1
  451.3 7.8 gather_fusion.3
  459.1 6.3 convolution_multiply_fusion
  465.4 1.8 select_select_fusion
  467.2 312.0 %all-reduce.8.cloned.1.call-done = (bf16[576,6912]{1,0:T(8,128)(2,1)}, bf16[1152,3,576]{0,2,1:T(8,128)(2,1)}, bf16[576,1152]{1,0:T(8,128)(2,1)}, bf16[1152,2304]{1,0:T(8,128)(2,1)}, bf16[2304,1152]{1,0:T(8,128)(2,1)}) async-done(((bf16[576,6912]{1,0:T(8,128)(2,1)}, bf16[1152,3,576]{0,2,1:T(8,128)(2,1)}, bf16[576,1152]{1,0:T(8,128)(2,1)}, bf16[1152,2304]{1,0:T(8,128)(2,1)}, bf16[2304,1152]{1,0:T(8,128)(2,1)}), ...) | async-done | bytes 23887888 | tf_op jit(solution)/shard_map/psum | solution.py:260
  779.2 3.2 convert_element_type.229
  782.4 10.4 %convert_element_type.221 = f32[576,6912]{1,0:T(8,128)} convert(bf16[576,6912]{1,0:T(8,128)(2,1)} %get-tuple-element.31) | non-fusion elementwise | flops 3981312 | bytes 23887872 | tf_op jit(solution)/shard_map/convert_element_type | solution.py:260
  792.8 6.0 convert_element_type.224
  798.8 4.9 convert_element_type.232
  803.8 4.8 convert_element_type.235
  (211 shorter events, 16.8 us)
Async XLA Ops:
  7.2 78.6 %copy-start = (bf16[576,1152]{1,0:T(8,128)(2,1)S(1)}, bf16[576,1152]{1,0:T(8,128)(2,1)}, u32[]{:S(2)}) copy-start(bf16[576,1152]{1,0:T(8,128)(2,1)} %param.27) | copy-start | bytes 3981316
  7.2 5.4 copy-start.42
  7.2 5.4 copy-start.57
  7.2 29.5 %all-reduce.6.cloned.1.call-start = ((), (), s32[]{:S(2)}) async-start(), calls=%async_computation.12 | async-start | bytes 221184
  7.3 5.6 copy-start.5
  12.5 57.6 %all-gather.6.cloned.1.call-start = ((), (), s32[]{:S(2)}) async-start(), calls=%async_computation.4 | async-start | bytes 2654208 | tf_op jit(solution)/shard_map/all_gather | solution.py:154
  12.7 5.9 copy-start.54
  12.8 25.5 %copy-start.31 = (pred[2,192]{1,0:T(4,128)(4,1)}, pred[2,192]{1,0:T(4,128)(4,1)S(1)}, u32[]{:S(2)}) copy-start(pred[2,192]{1,0:T(4,128)(4,1)S(1)} %iota_compare_fusion.2) | copy-start | bytes 1156
  12.9 6.7 copy-start.46
  12.9 6.8 copy-start.58
  18.6 21.9 %copy-start.9 = (bf16[384,1152]{1,0:T(8,128)(2,1)}, bf16[384,1152]{1,0:T(8,128)(2,1)S(1)}, u32[]{:S(2)}) copy-start(bf16[384,1152]{1,0:T(8,128)(2,1)S(1)} %gather_fusion) | copy-start | bytes 2654212
  18.6 22.1 %copy-start.53 = (bf16[2,576]{1,0:T(2,128)(2,1)S(1)}, bf16[2,576]{1,0:T(2,128)(2,1)}, u32[]{:S(2)}) copy-start(bf16[2,576]{1,0:T(2,128)(2,1)} %param.26) | copy-start | bytes 6916
  19.6 50.5 %copy-start.37 = (f32[2,192]{1,0:T(2,128)}, f32[2,192]{1,0:T(2,128)S(1)}, u32[]{:S(2)}) copy-start(f32[2,192]{1,0:T(2,128)S(1)} %add_rsqrt_fusion.1) | copy-start | bytes 4612
  40.5 76.8 %reduce-scatter.5.cloned.1.call-start = ((), (), s32[]{:S(2)}) async-start(), calls=%async_computation.5 | async-start | bytes 2654208 | tf_op jit(solution)/shard_map/reduce_scatter | solution.py:165
  40.9 39.4 %copy-start.44 = (f32[8,72]{1,0:T(8,128)}, f32[8,72]{1,0:T(8,128)S(1)}, u32[]{:S(2)}) copy-start(f32[8,72]{1,0:T(8,128)S(1)} %add.189) | copy-start | bytes 6916
  40.9 36.4 %copy-start.35 = (f32[8,72]{1,0:T(8,128)}, f32[8,72]{1,0:T(8,128)S(1)}, u32[]{:S(2)}) copy-start(f32[8,72]{1,0:T(8,128)S(1)} %add.192) | copy-start | bytes 6916
  77.3 3.0 copy-start.15
  79.1 3.3 copy-start.2
  85.8 2.9 copy-start.26
  85.8 3.4 copy-start.51
  88.8 63.3 %all-gather.8.cloned.1.call-start = ((), (), s32[]{:S(2)}) async-start(), calls=%async_computation.6 | async-start | bytes 2654208 | tf_op jit(solution)/shard_map/all_gather | solution.py:176
  97.1 21.6 %copy-start.28 = (f32[2,1152]{1,0:T(2,128)S(1)}, f32[2,1152]{1,0:T(2,128)}, u32[]{:S(2)}) copy-start(f32[2,1152]{1,0:T(2,128)} %get-tuple-element.42) | copy-start | bytes 27652
  97.1 21.6 %copy-start.32 = (pred[2,192]{1,0:T(4,128)(4,1)S(1)}, pred[2,192]{1,0:T(4,128)(4,1)}, u32[]{:S(2)}) copy-start(pred[2,192]{1,0:T(4,128)(4,1)} %copy-done.31) | copy-start | bytes 1156
  119.0 2.3 copy-start.34
  120.9 117.1 %copy-start.3 = (f32[2,192,1152]{2,1,0:T(8,128)}, f32[2,192,1152]{2,1,0:T(8,128)S(1)}, u32[]{:S(2)}) copy-start(f32[2,192,1152]{2,1,0:T(8,128)S(1)} %get-tuple-element.41) | copy-start | bytes 5308420
  122.6 61.0 %all-gather.10.cloned.1.call-start = ((), (), s32[]{:S(2)}) async-start(), calls=%async_computation.8 | async-start | bytes 2654208 | tf_op jit(solution)/shard_map/all_gather | solution.py:194
  123.2 110.7 %reduce-scatter.9.cloned.1.call-start = ((), (), s32[]{:S(2)}) async-start(), calls=%async_computation.9 | async-start | bytes 2654208 | tf_op jit(solution)/shard_map/reduce_scatter | solution.py:200
  123.3 120.1 %copy-start.47 = (f32[2304]{0:T(1024)}, f32[2304]{0:T(1024)S(1)}, u32[]{:S(2)}) copy-start(f32[2304]{0:T(1024)S(1)} %convert_element_type.199) | copy-start | bytes 27652
  205.4 67.3 %all-gather.12.cloned.1.call-start = ((), (), s32[]{:S(2)}) async-start(), calls=%async_computation.10 | async-start | bytes 2654208 | tf_op jit(solution)/shard_map/all_gather | solution.py:209
  235.4 2.7 copy-start.17
  235.4 2.7 copy-start.20
  240.6 2.8 copy-start.52
  243.1 96.0 %reduce-scatter.7.cloned.1.call-start = ((), (), s32[]{:S(2)}) async-start(), calls=%async_computation.7 | async-start | bytes 2654208 | tf_op jit(solution)/shard_map/reduce_scatter | solution.py:179
  255.4 24.0 %copy-start.45 = (f32[8,72]{1,0:T(8,128)S(1)}, f32[8,72]{1,0:T(8,128)}, u32[]{:S(2)}) copy-start(f32[8,72]{1,0:T(8,128)} %copy-done.44) | copy-start | bytes 6916
  255.4 94.3 %reduce-scatter.11.cloned.1.call-start = ((), (), s32[]{:S(2)}) async-start(), calls=%async_computation.11 | async-start | bytes 2654208 | tf_op jit(solution)/shard_map/reduce_scatter | solution.py:229
  276.4 9.3 %slice-start = ((s8[6291456]{0:T(1024)(128)(4,1)}), s8[2097152]{0:T(1024)(128)(4,1)S(1)}, s32[]{:S(2)}) async-start(s8[6291456]{0:T(1024)(128)(4,1)} %bitcast.139), calls=%async_computation.14 | async-start | bytes 4194304
  279.4 6.3 slice-start.1
  287.5 2.4 copy-start.36
  316.3 9.5 %copy-start.24 = (bf16[768,1152]{1,0:T(8,128)(2,1)S(1)}, bf16[768,1152]{1,0:T(8,128)(2,1)}, u32[]{:S(2)}) copy-start(bf16[768,1152]{1,0:T(8,128)(2,1)} %all-gather.10.cloned.1.call-done) | copy-start | bytes 5308420
  316.4 9.4 %copy-start.48 = (f32[2304]{0:T(1024)S(1)}, f32[2304]{0:T(1024)}, u32[]{:S(2)}) copy-start(f32[2304]{0:T(1024)} %copy-done.47) | copy-start | bytes 27652
  316.4 462.8 %all-reduce.8.cloned.1.call-start = ((), (), s32[]{:S(2)}) async-start(), calls=%async_computation.13 | async-start | bytes 47775744 | tf_op jit(solution)/shard_map/psum | solution.py:260
  341.2 8.6 %copy-start.18 = (f32[384,1152]{1,0:T(8,128)}, f32[384,1152]{1,0:T(8,128)S(1)}, u32[]{:S(2)}) copy-start(f32[384,1152]{1,0:T(8,128)S(1)} %convert_add_fusion) | copy-start | bytes 5308420
  341.2 2.6 copy-start.23
  341.2 3.4 copy-start.56
  344.6 5.2 copy-start.11
  344.6 5.2 copy-start.33
  344.6 5.2 copy-start.38
  349.8 3.5 copy-start.41
  349.8 3.5 copy-start.40
  349.8 3.5 copy-start.39
  349.8 8.1 copy-start.30
  363.5 2.9 copy-start.29
  368.0 8.6 %copy-start.6 = (bf16[2,256,1152]{2,1,0:T(8,128)(2,1)S(1)}, bf16[2,256,1152]{2,1,0:T(8,128)(2,1)}, u32[]{:S(2)}) copy-start(bf16[2,256,1152]{2,1,0:T(8,128)(2,1)} %param.19) | copy-start | bytes 3538948
  376.6 2.9 copy-start.14
  379.5 2.6 copy-start.22
  379.5 3.0 copy-start.50
  379.5 69.3 %copy-start.12 = (bf16[384,1152]{1,0:T(8,128)(2,1)S(1)}, bf16[384,1152]{1,0:T(8,128)(2,1)}, u32[]{:S(2)}) copy-start(bf16[384,1152]{1,0:T(8,128)(2,1)} %copy-done.9) | copy-start | bytes 2654212
  459.1 6.3 copy-start.8
  459.1 6.3 copy-start.21
  779.2 19.6 %slice-start.4 = ((s8[5308416]{0:T(1024)(128)(4,1)}), s8[4194304]{0:T(1024)(128)(4,1)S(1)}, s32[]{:S(2)}) async-start(s8[5308416]{0:T(1024)(128)(4,1)} %bitcast.159), calls=%async_computation.18 | async-start | bytes 8388608
  782.3 16.5 %slice-start.5 = ((s8[5308416]{0:T(1024)(128)(4,1)}), s8[1114112]{0:T(1024)(128)(4,1)S(1)}, s32[]{:S(2)}) async-start(s8[5308416]{0:T(1024)(128)(4,1)} %bitcast.159), calls=%async_computation.19 | async-start | bytes 2228224
  792.8 11.0 %slice-start.2 = ((s8[5308416]{0:T(1024)(128)(4,1)}), s8[4194304]{0:T(1024)(128)(4,1)S(1)}, s32[]{:S(2)}) async-start(s8[5308416]{0:T(1024)(128)(4,1)} %bitcast.157), calls=%async_computation.16 | async-start | bytes 8388608
  798.8 4.9 slice-start.3
  803.8 4.8 copy-start.1
  (12 other events, 19.6 us)
Sparse Core Ops, SparseCore 0:
  12.6 24.0 all-reduce.5
  40.6 29.4 all-gather.5
  88.9 28.3 reduce-scatter.4
  122.7 29.3 all-gather.7
  154.1 29.3 all-gather.9
  205.5 28.3 reduce-scatter.8
  243.2 29.3 all-gather.11
  274.9 28.3 reduce-scatter.6
  316.5 28.3 reduce-scatter.10
  363.6 415.5 all-reduce.7
where the time goes:
time: 821 us; the launch traced here: 816 us
  waiting for transfers between devices  473 us (58%)
  matrix products  128 us (16%)
  other arithmetic  73.6 us (9%)
  blocking collectives  67.8 us (8%)
  local copies, waits for them, and re-layouts  56.6 us (7%)
  between operations  15.8 us (2%)
    psum x1, waiting for transfers between devices, body(): lax.psum(grad_w_ada.astype(jnp.bfloat16), 'dp').astype(jnp.float32)  312 us
    psum x1, blocking collectives, body(): lax.psum(grad_b_ada.astype(jnp.bfloat16), 'dp').astype(jnp.float32)  63.3 us
    dot_general x5, matrix products, matmul_nn(): return jnp.dot(left_mat, right_mat, preferred_element_type=jnp.float32)  38.1 us
    dot_general x5, matrix products, matmul_nt(): lax.dot_general(left_mat, right_mat, (((1,), (1,)), ((), ())), preferred_...  38 us
    dot_general x5, matrix products, matmul_tn(): lax.dot_general(left_mat, right_mat, (((0,), (0,)), ((), ())), preferred_...  35.8 us
    all_gather x1, waiting for transfers between devices, body(): in_one_all = lax.all_gather(mod_in_one, 'tensor', axis=0, tiled=True)  29.1 us
    all_gather x1, waiting for transfers between devices, body(): in_two_all = lax.all_gather(mod_in_two, 'tensor', axis=0, tiled=True)  28.9 us
    reduce_scatter x1, waiting for transfers between devices, body(): lax.psum_scatter(matmul_nt(grad_pre, w_up).astype(jnp.bfloat16), 'tensor'...  28.4 us
  transfers between devices with their start and end apart: 10, of which 8 were waited for; matrix products, arithmetic and copies ran while one was open for 18% of the time, Pallas kernels for 0%

commit v1 on v0

v1 whole, which is shorter than its diff:
```python
import functools

import jax
import jax.numpy as jnp
from jax import lax
from jax.experimental import pallas as pl
from jax.experimental.pallas import tpu as pltpu
from jax.sharding import PartitionSpec as P

HD = 72
LANES = 128
NORM_EPS = 1e-06
MASKED = -1e30
GELU_C = 0.7978845608028654
GELU_A = 0.044715
F32 = jnp.float32
BF16 = jnp.bfloat16


def gelu_tanh(values):
    return 0.5 * values * (1.0 + jnp.tanh(GELU_C * (values + GELU_A * values * values * values)))


def gelu_slope(values):
    tanh_part = jnp.tanh(GELU_C * (values + GELU_A * values * values * values))
    return 0.5 * (1.0 + tanh_part) + 0.5 * values * (1.0 - tanh_part * tanh_part) * GELU_C * (
        1.0 + 3.0 * GELU_A * values * values
    )


def norm_rows(values):
    centre = values - jnp.mean(values, axis=-1, keepdims=True)
    inv_std = lax.rsqrt(jnp.mean(centre * centre, axis=-1, keepdims=True) + NORM_EPS)
    return (centre * inv_std, inv_std)


def norm_back(grad_norm, normed, inv_std):
    return inv_std * (
        grad_norm
        - jnp.mean(grad_norm, axis=-1, keepdims=True)
        - normed * jnp.mean(grad_norm * normed, axis=-1, keepdims=True)
    )


def matmul_nn(left_mat, right_mat):
    return jnp.dot(left_mat, right_mat, preferred_element_type=F32)


def matmul_tn(left_mat, right_mat):
    return lax.dot_general(left_mat, right_mat, (((0,), (0,)), ((), ())), preferred_element_type=F32)


def matmul_nt(left_mat, right_mat):
    return lax.dot_general(left_mat, right_mat, (((1,), (1,)), ((), ())), preferred_element_type=F32)


def head_window(head):
    first = head * HD // LANES * LANES
    last = -(-(head + 1) * HD // LANES) * LANES
    return first, last


def head_mask(head):
    first, last = head_window(head)
    cols = lax.broadcasted_iota(jnp.int32, (1, last - first), 1) + first
    return (cols >= head * HD) & (cols < (head + 1) * HD)


def pick(block_ref, base, head, mask=None):
    first, last = head_window(head)
    block = block_ref[:, base + first : base + last]
    if mask is None:
        return block
    return jnp.where(mask, block, jnp.zeros_like(block))


def add_tiles(tiles, head, block):
    first, last = head_window(head)
    for at in range(first, last, LANES):
        piece = block[:, at - first : at - first + LANES]
        tiles[at] = tiles[at] + piece if at in tiles else piece


def attend_kernel(heads, width, scale, counts_ref, qkv_ref, out_ref):
    rows = qkv_ref.shape[0]
    live = lax.broadcasted_iota(jnp.int32, (1, rows), 1) < counts_ref[pl.program_id(0)]
    tiles = {}
    for head in range(heads):
        mask = head_mask(head)
        scores = matmul_nt(pick(qkv_ref, 0, head, mask), pick(qkv_ref, width, head)) * scale
        scores = jnp.where(live, scores, MASKED)
        exp_scores = jnp.exp(scores - jnp.max(scores, axis=-1, keepdims=True))
        probs = exp_scores / jnp.sum(exp_scores, axis=-1, keepdims=True)
        add_tiles(tiles, head, matmul_nn(probs.astype(BF16), pick(qkv_ref, 2 * width, head, mask)))
    for at, tile in tiles.items():
        out_ref[:, at : at + LANES] = tile.astype(BF16)


def attend_back_kernel(heads, width, scale, counts_ref, qkv_ref, datt_ref, out_ref):
    rows = qkv_ref.shape[0]
    live = lax.broadcasted_iota(jnp.int32, (rows, 1), 0) < counts_ref[pl.program_id(0)]
    tiles = ({}, {}, {})
    for head in range(heads):
        mask = head_mask(head)
        queries = pick(qkv_ref, 0, head, mask)
        key_rows = pick(qkv_ref, width, head, mask)
        grad_att = pick(datt_ref, 0, head, mask)
        scores = jnp.where(live, matmul_nt(key_rows, queries) * scale, MASKED)
        exp_scores = jnp.exp(scores - jnp.max(scores, axis=0, keepdims=True))
        probs = exp_scores / jnp.sum(exp_scores, axis=0, keepdims=True)
        grad_probs = matmul_nt(pick(qkv_ref, 2 * width, head), grad_att)
        inner = jnp.sum(probs * grad_probs, axis=0, keepdims=True)
        grad_scores = (probs * (grad_probs - inner)).astype(BF16)
        add_tiles(tiles[0], head, matmul_tn(grad_scores, key_rows) * scale)
        add_tiles(tiles[1], head, matmul_nn(grad_scores, queries) * scale)
        add_tiles(tiles[2], head, matmul_nn(probs.astype(BF16), grad_att))
    for part in range(3):
        for at, tile in tiles[part].items():
            out_ref[:, part * width + at : part * width + at + LANES] = tile.astype(BF16)


def attend_cost(images, rows, heads, products):
    return pl.CostEstimate(
        flops=2 * products * images * heads * rows * rows * 256,
        bytes_accessed=images * rows * heads * HD * 2 * 8,
        transcendentals=images * heads * rows * rows,
    )


def attend(qkv, counts, rows, heads, width, scale):
    images = counts.shape[0]
    return pl.pallas_call(
        functools.partial(attend_kernel, heads, width, scale),
        grid_spec=pltpu.PrefetchScalarGridSpec(
            num_scalar_prefetch=1,
            grid=(images,),
            in_specs=[pl.BlockSpec((rows, 3 * width), lambda i, c: (i, 0))],
            out_specs=pl.BlockSpec((rows, width), lambda i, c: (i, 0)),
        ),
        out_shape=jax.ShapeDtypeStruct((images * rows, width), BF16),
        cost_estimate=attend_cost(images, rows, heads, 2),
        name="attend",
    )(counts, qkv)


def attend_back(qkv, grad_att, counts, rows, heads, width, scale):
    images = counts.shape[0]
    return pl.pallas_call(
        functools.partial(attend_back_kernel, heads, width, scale),
        grid_spec=pltpu.PrefetchScalarGridSpec(
            num_scalar_prefetch=1,
            grid=(images,),
            in_specs=[
                pl.BlockSpec((rows, 3 * width), lambda i, c: (i, 0)),
                pl.BlockSpec((rows, width), lambda i, c: (i, 0)),
            ],
            out_specs=pl.BlockSpec((rows, 3 * width), lambda i, c: (i, 0)),
        ),
        out_shape=jax.ShapeDtypeStruct((images * rows, 3 * width), BF16),
        cost_estimate=attend_cost(images, rows, heads, 5),
        name="attend_back",
    )(counts, qkv, grad_att)


def from_peer(value, size):
    return lax.ppermute(value, "tensor", [((i + 1) % size, i) for i in range(size)])


def gather_chunks(value, size):
    if size == 1:
        return [value]
    if size == 2:
        return [value, from_peer(value, size)]
    whole = lax.all_gather(value, "tensor", axis=0)
    whole = jnp.roll(whole, -lax.axis_index("tensor"), axis=0)
    return [whole[k] for k in range(size)]


def whole_sums(parts, size):
    if size == 1:
        return [parts[0].astype(F32)]
    if size == 2:
        return [
            parts[0].astype(F32) + from_peer(parts[1], size).astype(F32),
            parts[1].astype(F32) + from_peer(parts[0], size).astype(F32),
        ]
    me = lax.axis_index("tensor")
    whole = lax.psum(jnp.roll(jnp.stack(parts), me, axis=0), "tensor")
    whole = jnp.roll(whole, -me, axis=0).astype(F32)
    return [whole[k] for k in range(size)]


def own_sum(parts, size):
    if size == 1:
        return parts[0]
    if size == 2:
        return parts[0] + from_peer(parts[1].astype(BF16), size).astype(F32)
    me = lax.axis_index("tensor")
    whole = jnp.roll(jnp.stack(parts).astype(BF16), me, axis=0)
    return lax.psum_scatter(whole, "tensor", scatter_dimension=0, tiled=False).astype(F32)


def closed_path(chips):
    deep = 4 if chips % 4 == 0 else 1
    wide = chips // deep
    path = [(0, 0)] if wide > 1 else []
    for row in range(deep):
        line = range(min(1, wide - 1), wide)
        path += [(row, col) for col in (line if row % 2 == 0 else reversed(line))]
    if wide > 1:
        path += [(row, 0) for row in range(deep - 1, 0, -1)]
    return [row * wide + col for row, col in path]


class Ring:
    def __init__(self, groups, flip=False):
        self.groups, self.chips = groups, groups // 2
        self.usable = groups % 2 == 0 and self.chips >= 3
        if not self.usable:
            return
        self.path = closed_path(self.chips)
        if flip:
            self.path = self.path[::-1]
        self.far = self.chips // 2
        self.near = self.chips - 1 - self.far
        me = lax.axis_index("dp")
        self.core = me % 2
        place = [self.path.index(chip) for chip in range(self.chips)]
        self.spot = jnp.asarray(place, jnp.int32)[me // 2]

    def hop(self, value, step):
        path = self.path
        pairs = [
            (2 * path[n] + c, 2 * path[(n + step) % self.chips] + c)
            for n in range(self.chips)
            for c in (0, 1)
        ]
        return lax.ppermute(value, "dp", pairs)

    def partner(self, value):
        return lax.ppermute(value, "dp", [(n, n ^ 1) for n in range(self.groups)])

    def at(self, ahead):
        return lax.rem(self.spot + ahead + self.chips, self.chips)

    def spread(self, value):
        found = [(0, value)]
        front = back = value
        for ahead in range(1, self.far + 1):
            if ahead <= self.near:
                front = self.hop(front, 1)
                found.append((-ahead, front))
            back = self.hop(back, -1)
            found.append((ahead, back))
        return found

    def gather(self, value):
        if not self.usable:
            return lax.all_gather(value, "dp", axis=0)
        column = jnp.stack([piece for _, piece in self.spread(value)])
        return jnp.concatenate([column, self.partner(column)])

    def sum(self, mat):
        height, breadth = mat.shape
        if not self.usable or height % (8 * self.groups):
            return lax.psum(mat, "dp")

        def added(*terms):
            return sum(term.astype(F32) for term in terms).astype(BF16)

        halves = mat.reshape(2, self.chips, height // self.groups, breadth)
        half = lambda which: lax.dynamic_index_in_dim(halves, which, 0, keepdims=False)
        held = added(half(self.core), self.partner(half(1 - self.core)))
        block = lambda ahead: lax.dynamic_index_in_dim(held, self.at(ahead), 0, keepdims=False)
        front, back = block(self.far), block(-self.near)
        for left in range(self.far - 1, 0, -1):
            front = added(self.hop(front, 1), block(left))
            if left < self.near:
                back = added(self.hop(back, -1), block(-left))
        whole = added(block(0), self.hop(front, 1), self.hop(back, -1))
        summed = jnp.zeros_like(held)
        for ahead, value in self.spread(whole):
            summed = lax.dynamic_update_index_in_dim(summed, value, self.at(ahead), 0)
        other = self.partner(summed)
        first = jnp.where(self.core == 0, summed, other)
        second = jnp.where(self.core == 0, other, summed)
        return jnp.concatenate([first, second]).reshape(height, breadth)


def body(
    size,
    groups,
    tokens,
    condition,
    keep_count,
    token_order,
    w_ada,
    b_ada,
    w_qkv,
    b_qv,
    w_proj,
    b_proj,
    w_up,
    b_up,
    w_down,
    b_down,
    cotangent,
):
    own, seq, feat = tokens.shape
    kept = 3 * seq // 4
    rows = own * kept
    cols = w_qkv.shape[2]
    heads = cols // HD
    width = -(-cols // LANES) * LANES
    scale = HD ** (-0.5)
    me = lax.axis_index("tensor")
    chunks = range(size)
    ring, back_ring = Ring(groups), Ring(groups, flip=True)

    counts = jnp.roll(keep_count, -me * own)
    own_counts = counts[:own]
    chunk_counts = [counts[k * own : (k + 1) * own] for k in chunks]

    slots = jnp.arange(kept, dtype=jnp.int32)
    places = jnp.arange(seq, dtype=jnp.int32)
    chosen = (token_order[:, :kept, None] == places) & (
        slots[None, :, None] < own_counts[:, None, None]
    )
    select = chosen.astype(BF16)
    kept_pos = jnp.any(chosen, axis=1)

    def picked(values):
        return jnp.einsum("isp,ipd->isd", select, values, preferred_element_type=F32).astype(BF16)

    x_chunks = gather_chunks(picked(tokens), size)
    cot_chunks = gather_chunks(picked(cotangent), size)

    cond = jnp.roll(condition, -me * own, axis=0).astype(F32)
    silu_cond = jax.nn.silu(cond).astype(BF16)
    mod_part = matmul_nn(silu_cond, w_ada)
    mod_sum = whole_sums([mod_part[k * own : (k + 1) * own] for k in chunks], size)
    mods = [
        [block[:, None, :] for block in jnp.split(mod_sum[k] + b_ada.astype(F32), 6, axis=1)]
        for k in chunks
    ]

    qkv_weight = jnp.pad(w_qkv, ((0, 0), (0, 0), (0, width - cols))).reshape(feat, 3 * width)
    proj_weight = jnp.pad(w_proj, ((0, width - cols), (0, 0)))
    bias_q, bias_v = b_qv.astype(F32)
    zero_pad = jnp.zeros((width - cols,), F32)
    qkv_bias = jnp.concatenate(
        [bias_q, zero_pad, jnp.zeros((width,), F32), bias_v, zero_pad]
    )

    def flat(values):
        return values.reshape(rows, feat)

    def images(values):
        return values.reshape(own, kept, feat)

    in_one, qkv, att, proj_part, normed_one, inv_one = ([None] * size for _ in range(6))
    for k in chunks:
        shift_one, scale_one = mods[k][0], mods[k][1]
        normed_one[k], inv_one[k] = norm_rows(x_chunks[k].astype(F32))
        in_one[k] = flat((normed_one[k] * (1.0 + scale_one) + shift_one).astype(BF16))
        qkv[k] = (matmul_nn(in_one[k], qkv_weight) + qkv_bias).astype(BF16)
        att[k] = attend(qkv[k], chunk_counts[k], kept, heads, width, scale)
        proj_part[k] = matmul_nn(att[k], proj_weight).astype(BF16)
    proj_sum = whole_sums(proj_part, size)

    branch_one, normed_two, inv_two, in_two, grad_two, hidden, resid = (
        [None] * size for _ in range(7)
    )
    grad_branch_two, grad_pre, down_part, up_part = ([None] * size for _ in range(4))
    for k in reversed(chunks):
        gate_one, shift_two, scale_two, gate_two = mods[k][2:]
        branch_one[k] = images(proj_sum[k] + b_proj.astype(F32))
        resid[k] = x_chunks[k].astype(F32) + gate_one * branch_one[k]
        normed_two[k], inv_two[k] = norm_rows(resid[k])
        in_two[k] = flat((normed_two[k] * (1.0 + scale_two) + shift_two).astype(BF16))
        pre_act = matmul_nn(in_two[k], w_up) + b_up.astype(F32)
        grad_two[k] = cot_chunks[k].astype(F32)
        grad_branch_two[k] = flat((gate_two * grad_two[k]).astype(BF16))
        grad_pre[k] = (matmul_nt(grad_branch_two[k], w_down) * gelu_slope(pre_act)).astype(BF16)
        up_part[k] = matmul_nt(grad_pre[k], w_up).astype(BF16)
        hidden[k] = gelu_tanh(pre_act).astype(BF16)
        down_part[k] = matmul_nn(hidden[k], w_down)
    grad_in_two = whole_sums(up_part, size)

    hidden_all = jnp.concatenate(hidden)
    grad_branch_two_all = jnp.concatenate(grad_branch_two)
    grad_pre_all = jnp.concatenate(grad_pre)
    grad_w_down = matmul_tn(hidden_all, grad_branch_two_all).astype(BF16)
    grad_w_up = matmul_tn(jnp.concatenate(in_two), grad_pre_all).astype(BF16)
    (grad_two, grad_w_down, grad_w_up) = lax.optimization_barrier(
        (grad_two, grad_w_down, grad_w_up)
    )
    grad_w_down, grad_w_up = ring.sum(grad_w_down), back_ring.sum(grad_w_up)
    grad_b_down = jnp.sum(grad_branch_two_all, axis=0, dtype=F32)
    grad_b_up = jnp.sum(grad_pre_all, axis=0, dtype=F32)

    branch_two = images(own_sum(down_part, size) + b_down.astype(F32))
    resid_two = (resid[0] + mods[0][5] * branch_two).astype(BF16)
    placed_out = jnp.einsum("isp,isd->ipd", select, resid_two, preferred_element_type=F32)
    block_out = jnp.where(kept_pos[:, :, None], placed_out.astype(BF16), tokens)
    grad_gate_two = jnp.sum(grad_two[0] * branch_two, axis=1)

    grad_one, grad_branch_one, grad_qkv, one_part = ([None] * size for _ in range(4))
    for k in chunks:
        gate_one, scale_two = mods[k][2], mods[k][4]
        grad_in = images(grad_in_two[k])
        grad_one[k] = grad_two[k] + norm_back(
            grad_in * (1.0 + scale_two), normed_two[k], inv_two[k]
        )
        grad_branch_one[k] = flat((gate_one * grad_one[k]).astype(BF16))
        grad_att = matmul_nt(grad_branch_one[k], proj_weight).astype(BF16)
        grad_qkv[k] = attend_back(
            qkv[k], grad_att, chunk_counts[k], kept, heads, width, scale
        )
        one_part[k] = matmul_nt(grad_qkv[k], qkv_weight)
    grad_in_one = images(own_sum(one_part, size))

    grad_branch_one_all = jnp.concatenate(grad_branch_one)
    grad_qkv_all = jnp.concatenate(grad_qkv)
    grad_w_proj = matmul_tn(grad_branch_one_all, jnp.concatenate(att)).astype(BF16)
    grad_w_qkv = matmul_tn(jnp.concatenate(in_one), grad_qkv_all).astype(BF16)
    grad_w_att = ring.sum(jnp.concatenate([grad_w_qkv, grad_w_proj], axis=1))
    grad_w_att = grad_w_att.astype(F32).reshape(feat, 4, width)[:, :, :cols]
    grad_b_proj = jnp.sum(grad_branch_one_all, axis=0, dtype=F32)
    grad_b_qkv = jnp.sum(grad_qkv_all, axis=0, dtype=F32)

    grad_mid = images(grad_in_two[0])
    grad_shift_two = jnp.sum(grad_mid, axis=1)
    grad_scale_two = jnp.sum(grad_mid * normed_two[0], axis=1)
    grad_gate_one = jnp.sum(grad_one[0] * branch_one[0], axis=1)
    grad_shift_one = jnp.sum(grad_in_one, axis=1)
    grad_scale_one = jnp.sum(grad_in_one * normed_one[0], axis=1)
    grad_rows = grad_one[0] + norm_back(
        grad_in_one * (1.0 + mods[0][1]), normed_one[0], inv_one[0]
    )
    high = lax.reduce_precision(grad_rows, 8, 7)
    placed_grad = jnp.einsum(
        "isp,isd->ipd", select, high.astype(BF16), preferred_element_type=F32
    ) + jnp.einsum(
        "isp,isd->ipd", select, (grad_rows - high).astype(BF16), preferred_element_type=F32
    )
    grad_tokens = jnp.where(kept_pos[:, :, None], placed_grad, cotangent.astype(F32))

    grad_mod = jnp.concatenate(
        [
            grad_shift_one,
            grad_scale_one,
            grad_gate_one,
            grad_shift_two,
            grad_scale_two,
            grad_gate_two,
        ],
        axis=1,
    ).astype(BF16)
    grad_mod = jnp.concatenate(gather_chunks(grad_mod, size))
    sigmoid_c = jax.nn.sigmoid(cond)
    grad_condition = matmul_nt(grad_mod, w_ada) * (sigmoid_c * (1.0 + cond * (1.0 - sigmoid_c)))
    grad_condition = jnp.roll(grad_condition, me * own, axis=0)

    biases = jnp.concatenate(
        [grad_b_qkv[:cols], grad_b_qkv[2 * width : 2 * width + cols], grad_b_proj, grad_b_up, grad_b_down]
    ).astype(BF16)
    pieces = [grad_mod.reshape(-1), silu_cond.reshape(-1), biases]
    packed = ring.gather(jnp.concatenate(pieces))
    first, second = pieces[0].size, pieces[0].size + pieces[1].size
    grad_mod_all = packed[:, :first].reshape(-1, 6 * feat)
    silu_all = packed[:, first:second].reshape(-1, silu_cond.shape[1])
    bias_sums = jnp.sum(packed[:, second:], axis=0, dtype=F32)
    grad_w_ada = matmul_tn(silu_all, grad_mod_all)
    grad_b_ada = jnp.sum(grad_mod_all, axis=0, dtype=F32)
    hid = w_up.shape[1]
    cuts = [0, 2 * cols, 2 * cols + feat, 2 * cols + feat + hid, 2 * cols + 2 * feat + hid]
    grad_b_qv, grad_b_proj, grad_b_up, grad_b_down = (
        bias_sums[cuts[n] : cuts[n + 1]] for n in range(4)
    )
    return (
        block_out,
        grad_tokens,
        grad_condition,
        grad_w_ada,
        grad_b_ada,
        grad_w_att[:, :3],
        grad_b_qv.reshape(2, cols),
        grad_w_att[:, 3].T,
        grad_b_proj,
        grad_w_up.astype(F32),
        grad_b_up,
        grad_w_down.astype(F32),
        grad_b_down,
    )


def solution(mesh):
    placed = (
        P(("dp", "tensor"), None, None),
        P("dp", "tensor"),
        P("dp"),
        P(("dp", "tensor"), None),
        P("tensor", None),
        P(),
        P(None, None, "tensor"),
        P(None, "tensor"),
        P("tensor", None),
        P(),
        P(None, "tensor"),
        P("tensor"),
        P("tensor", None),
        P(),
        P(("dp", "tensor"), None, None),
    )
    return jax.shard_map(
        functools.partial(body, mesh.shape["tensor"], mesh.shape["dp"]),
        mesh=mesh,
        in_specs=placed,
        out_specs=(
            P(("dp", "tensor"), None, None),
            P(("dp", "tensor"), None, None),
            P("dp", "tensor"),
            P("tensor", None),
            P(),
            P(None, None, "tensor"),
            P(None, "tensor"),
            P("tensor", None),
            P(),
            P(None, "tensor"),
            P("tensor"),
            P("tensor", None),
            P(),
        ),
        check_vma=False,
    )
```

time: 821 us -> 560 us (0.68)
  waiting for transfers between devices: 473 us -> 143 us
  blocking collectives: 67.8 us -> 0 us
  starting transfers between devices: 1.17 us -> 63.3 us
  local copies, waits for them, and re-layouts: 56.6 us -> 99.1 us
  Pallas kernels: 0 us -> 29.4 us
  other arithmetic: 73.6 us -> 92 us
  matrix products: 128 us -> 110 us
    psum x1 -> x0, waiting for transfers between devices: 312 us -> none  [body(): lax.psum(grad_w_ada.astype(jnp.bfloat16), 'dp').astype(jnp.float32)]
    ppermute x0 -> x67, waiting for transfers between devices: none -> 143 us  [the longest x49 107 us: hop(): return lax.ppermute(value, 'dp', pairs)]
    all_gather x4 -> x0, waiting for transfers between devices: 95.8 us -> none  [the longest x1 29.1 us: body(): in_one_all = lax.all_gather(mod_in_one, 'tensor', axis=0, tiled=True)]
    psum x1 -> x0, blocking collectives: 63.3 us -> none  [body(): lax.psum(grad_b_ada.astype(jnp.bfloat16), 'dp').astype(jnp.float32)]
    ppermute x0 -> x67, starting transfers between devices: none -> 63.3 us  [the longest x49 50.2 us: hop(): return lax.ppermute(value, 'dp', pairs)]
    reduce_scatter x4 -> x0, waiting for transfers between devices: 48.6 us -> none  [the longest x1 28.4 us: body(): lax.psum_scatter(matmul_nt(grad_pre, w_up).astype(jnp.bfloat16), 'tensor'...]
    pallas_call x0 -> x4, Pallas kernels: none -> 29.4 us  [the longest x2 18.6 us: attend_back(): pl.pallas_call(functools.partial(attend_back_kernel, heads, width, scale)...]
    gather x5 -> x0, local copies, waits for them, and re-layouts: 29.2 us -> none  [the longest x1 8.57 us: body(): out_rows = jnp.take_along_axis(resid_two, rank_slot[:, :, None], axis=1)]
  transfers between devices with their start and end apart: 10 -> 67, of which waited for: 8 -> 25; matrix products, arithmetic and copies ran while one was open for 18% -> 40% of each run, Pallas kernels for 0% -> 5%
where the time goes in v1:
time: 560 us; the launch traced here: 549 us
  waiting for transfers between devices  143 us (26%)
  matrix products  110 us (20%)
  local copies, waits for them, and re-layouts  99.1 us (18%)
  other arithmetic  92 us (16%)
  starting transfers between devices  63.3 us (11%)
  Pallas kernels  29.4 us (5%)
  between operations  13.1 us (2%)
    ppermute x49, waiting for transfers between devices, hop(): return lax.ppermute(value, 'dp', pairs)  107 us
    ppermute x49, starting transfers between devices, hop(): return lax.ppermute(value, 'dp', pairs)  50.2 us
    ppermute x11, waiting for transfers between devices, from_peer(): lax.ppermute(value, 'tensor', [((i + 1) % size, i) for i in range(size)])  35.6 us
    dot_general x9, matrix products, matmul_nn(): return jnp.dot(left_mat, right_mat, preferred_element_type=F32)  34.9 us
    dot_general x9, matrix products, matmul_nt(): lax.dot_general(left_mat, right_mat, (((1,), (1,)), ((), ())), preferred_...  33.3 us
    dot_general x5, matrix products, matmul_tn(): lax.dot_general(left_mat, right_mat, (((0,), (0,)), ((), ())), preferred_...  29.8 us
    unnamed x210, local copies, waits for them, and re-layouts  21.5 us
    convert_element_type x12, other arithmetic, added(): return sum((term.astype(F32) for term in terms)).astype(BF16)  18.7 us
  transfers between devices with their start and end apart: 67, of which 25 were waited for; matrix products, arithmetic and copies ran while one was open for 40% of the time, Pallas kernels for 5%

profile of v1, /device:TPU:0, one launch (start us, length us, event | category | flops | bytes accessed | tf_op | source)
XLA Modules:
  0.0 549.3 jit_solution(12706909251146993839)
XLA Ops:
  1.6 4.6 fusion.145
  6.2 3.0 collective-permute-start
  14.3 2.4 pad.8
  18.7 4.0 fusion.132
  24.8 3.4 add_convert_fusion.1.qkv_ref
  28.2 5.2 attend.2
  33.4 3.3 convolution_convert_fusion.12
  40.3 5.9 %add_convert_fusion.qkv_ref = bf16[384,1920]{1,0:T(8,128)(2,1)} fusion(bf16[384,1152]{1,0:T(8,128)(2,1)S(1)} %bitcast.266, bf16[1152,1920]{0,1:T(8,128)(2,1)} %bitcast.230, f32[1920]{0:T(1024)S(1)} %copy-done.84), kind=kOutput, calls=%fused_computation.51 | convolution fusion | flops 1700167680 | bytes 6790656 | tf_op jit(solution)/shard_map/dot_general | solution.py:46
  46.2 5.6 %attend.3 = bf16[384,640]{1,0:T(8,128)(2,1)} custom-call(s32[2]{0:T(128)} %get-tuple-element.142.counts_ref, bf16[384,1920]{1,0:T(8,128)(2,1)} %add_convert_fusion.qkv_ref), custom_call_target="tpu_custom_call" | custom-call | flops 603979776 | bytes 3538944 | tf_op jit(solution)/shard_map/attend/pallas_call | solution.py:132
  77.5 11.9 %collective-permute-done.3 = bf16[384,1152]{1,0:T(8,128)(2,1)} collective-permute-done((bf16[384,1152]{1,0:T(8,128)(2,1)S(1)}, bf16[384,1152]{1,0:T(8,128)(2,1)}, u32[]{:S(2)}, u32[]{:S(2)}) %collective-permute-start.3) | collective-permute-done | bytes 884768 | tf_op jit(solution)/shard_map/ppermute | solution.py:166
  95.3 4.2 multiply_convert_fusion.1
  99.5 2.9 multiply_convert_fusion
  102.4 3.8 fusion.144
  106.3 2.5 convolution_convert_fusion.6
  108.8 3.4 convolution_convert_fusion.9
  114.2 3.6 fusion.143
  117.8 5.3 convolution_convert_fusion
  123.1 8.7 %convolution_convert_fusion.1 = bf16[2304,1152]{1,0:T(8,128)(2,1)S(1)} fusion(bf16[384,2304]{1,0:T(8,128)(2,1)} %copy-done.93, bf16[384,2304]{1,0:T(8,128)(2,1)} %get-tuple-element.146, bf16[384,1152]{1,0:T(8,128)(2,1)S(1)} %bitcast.257, bf16[384,1152]{1,0:T(8,128)(2,1)S(1)} %bitcast.255), kind=kOutput, calls=%fused_computation.1 | convolution fusion | flops 4090134528 | bytes 10616832 | tf_op jit(solution)/shard_map/dot_general | solution.py:50
  137.8 13.8 %collective-permute-done.7 = bf16[384,1152]{1,0:T(8,128)(2,1)S(1)} collective-permute-done((bf16[384,1152]{1,0:T(8,128)(2,1)S(1)}, bf16[384,1152]{1,0:T(8,128)(2,1)S(1)}, u32[]{:S(2)}, u32[]{:S(2)}) %collective-permute-start.7) | collective-permute-done | bytes 884768 | tf_op jit(solution)/shard_map/ppermute | solution.py:166
  151.6 4.0 fusion.61
  157.5 2.9 multiply_reduce_fusion.1
  161.9 3.4 fusion.134
  168.1 4.8 add_add_fusion
  172.9 9.4 %attend_back.2 = bf16[384,1920]{1,0:T(8,128)(2,1)} custom-call(s32[2]{0:T(128)} %copy-done.86, bf16[384,1920]{1,0:T(8,128)(2,1)} %add_convert_fusion.1.qkv_ref, bf16[384,640]{1,0:T(8,128)(2,1)} %convolution_convert_fusion.14.datt_ref), custom_call_target="tpu_custom_call" | custom-call | flops 1509949440 | bytes 3538944 | tf_op jit(solution)/shard_map/attend_back/pallas_call | solution.py:148
  184.6 2.9 multiply_reduce_fusion
  198.4 2.7 convolution_convert_fusion.3
  202.8 9.2 %attend_back.3 = bf16[384,1920]{1,0:T(8,128)(2,1)} custom-call(s32[2]{0:T(128)} %get-tuple-element.142.counts_ref, bf16[384,1920]{1,0:T(8,128)(2,1)} %add_convert_fusion.qkv_ref, bf16[384,640]{1,0:T(8,128)(2,1)} %convolution_convert_fusion.13.datt_ref), custom_call_target="tpu_custom_call" | custom-call | flops 1509949440 | bytes 3538944 | tf_op jit(solution)/shard_map/attend_back/pallas_call | solution.py:148
  212.0 5.9 %convolution_convert_fusion.5 = bf16[384,1152]{1,0:T(8,128)(2,1)} fusion(bf16[384,1920]{1,0:T(8,128)(2,1)} %attend_back.3, bf16[1152,1920]{0,1:T(8,128)(2,1)} %bitcast.231), kind=kOutput, calls=%fused_computation.56 | convolution fusion | flops 1699135488 | bytes 6782976 | tf_op jit(solution)/shard_map/dot_general | solution.py:54
  218.0 4.1 convolution_convert_fusion.2
  222.8 3.1 pad_maximum_fusion
  227.5 3.7 dynamic-slice_bitcast_fusion
  231.3 9.9 %collective-permute-done.9 = bf16[384,1152]{1,0:T(8,128)(2,1)S(1)} collective-permute-done((bf16[384,1152]{1,0:T(8,128)(2,1)}, bf16[384,1152]{1,0:T(8,128)(2,1)S(1)}, u32[]{:S(2)}, u32[]{:S(2)}) %collective-permute-start.9) | collective-permute-done | bytes 884768 | tf_op jit(solution)/shard_map/ppermute | solution.py:166
  241.2 4.5 fusion.59
  249.0 2.7 fusion.70
  251.7 2.5 fusion.21
  254.3 2.5 fusion.1
  261.4 3.2 fusion.2
  265.3 2.5 collective-permute-done.12
  273.1 5.4 convolution_multiply_fusion.2
  287.3 4.9 stack.35
  296.6 7.0 %collective-permute-done.53 = bf16[144,1152]{1,0:T(8,128)(2,1)S(1)} collective-permute-done((bf16[144,1152]{1,0:T(8,128)(2,1)S(1)}, bf16[144,1152]{1,0:T(8,128)(2,1)S(1)}, u32[]{:S(2)}, u32[]{:S(2)}) %collective-permute-start.53) | collective-permute-done | bytes 331808 | tf_op jit(solution)/shard_map/ppermute | solution.py:238
  311.8 8.4 %concatenate.81 = bf16[16,35712]{1,0:T(8,128)(2,1)} concatenate(bf16[1,35712]{1,0:T(2,128)(2,1)S(1)} %stack.27, bf16[1,35712]{1,0:T(2,128)(2,1)S(1)} %stack.28, bf16[1,35712]{1,0:T(2,128)(2,1)S(1)} %stack.29, bf16[1,35712]{1,0:T(2,128)(2,1)S(1)} %stack.30, bf16[1,35712]{1,0:T(2,128)(2,1)S(1)} %stack.31, bf16[1,35712]{1,0:T(2,128)(2,1)} %stack.32, bf16[1,35712]{1,0:T(2,128)(2,1)S(1)} %stack.33, ...), dimensions={0} | concatenate | bytes 2285568 | tf_op jit(solution)/shard_map/concatenate | solution.py:261
  329.0 9.0 %fusion.146 = f32[576,6912]{1,0:T(8,128)} fusion(bf16[64,576]{1,0:T(8,128)(2,1)} %reshape.347, bf16[64,6912]{1,0:T(8,128)(2,1)S(1)} %reshape.348), kind=kOutput, calls=%fused_computation.305 | convolution fusion | flops 509607936 | bytes 16883712 | tf_op jit(solution)/shard_map/dot_general | solution.py:50
  344.9 5.1 collective-permute-done.55
  354.3 4.0 collective-permute-done.39
  366.5 6.2 %collective-permute-done.43 = bf16[72,2304]{1,0:T(8,128)(2,1)} collective-permute-done((bf16[72,2304]{1,0:T(8,128)(2,1)}, bf16[72,2304]{1,0:T(8,128)(2,1)}, u32[]{:S(2)}, u32[]{:S(2)}) %collective-permute-start.43) | collective-permute-done | bytes 331808 | tf_op jit(solution)/shard_map/ppermute | solution.py:238
  382.5 4.3 collective-permute-done.45
  390.6 3.5 fusion
  396.3 4.7 collective-permute-done.47
  403.1 6.6 %collective-permute-done.20 = bf16[72,2560]{1,0:T(8,128)(2,1)S(1)} collective-permute-done((bf16[72,2560]{1,0:T(8,128)(2,1)S(1)}, bf16[72,2560]{1,0:T(8,128)(2,1)S(1)}, u32[]{:S(2)}, u32[]{:S(2)}) %collective-permute-start.20) | collective-permute-done | bytes 368672 | tf_op jit(solution)/shard_map/ppermute | solution.py:238
  411.1 10.6 %collective-permute-done.21 = bf16[72,2560]{1,0:T(8,128)(2,1)S(1)} collective-permute-done((bf16[72,2560]{1,0:T(8,128)(2,1)S(1)}, bf16[72,2560]{1,0:T(8,128)(2,1)S(1)}, u32[]{:S(2)}, u32[]{:S(2)}) %collective-permute-start.21) | collective-permute-done | bytes 368672 | tf_op jit(solution)/shard_map/ppermute | solution.py:238
  424.0 8.1 %collective-permute-done.22 = bf16[72,2560]{1,0:T(8,128)(2,1)S(1)} collective-permute-done((bf16[72,2560]{1,0:T(8,128)(2,1)S(1)}, bf16[72,2560]{1,0:T(8,128)(2,1)S(1)}, u32[]{:S(2)}, u32[]{:S(2)}) %collective-permute-start.22) | collective-permute-done | bytes 368672 | tf_op jit(solution)/shard_map/ppermute | solution.py:238
  436.1 7.2 %collective-permute-done.23 = bf16[72,2560]{1,0:T(8,128)(2,1)S(1)} collective-permute-done((bf16[72,2560]{1,0:T(8,128)(2,1)S(1)}, bf16[72,2560]{1,0:T(8,128)(2,1)S(1)}, u32[]{:S(2)}, u32[]{:S(2)}) %collective-permute-start.23) | collective-permute-done | bytes 368672 | tf_op jit(solution)/shard_map/ppermute | solution.py:238
  445.9 7.9 %collective-permute-done.27 = bf16[72,2560]{1,0:T(8,128)(2,1)S(1)} collective-permute-done((bf16[72,2560]{1,0:T(8,128)(2,1)S(1)}, bf16[72,2560]{1,0:T(8,128)(2,1)S(1)}, u32[]{:S(2)}, u32[]{:S(2)}) %collective-permute-start.27) | collective-permute-done | bytes 368672 | tf_op jit(solution)/shard_map/ppermute | solution.py:238
  456.8 6.9 %collective-permute-done.29 = bf16[72,2560]{1,0:T(8,128)(2,1)S(1)} collective-permute-done((bf16[72,2560]{1,0:T(8,128)(2,1)S(1)}, bf16[72,2560]{1,0:T(8,128)(2,1)S(1)}, u32[]{:S(2)}, u32[]{:S(2)}) %collective-permute-start.29) | collective-permute-done | bytes 368672 | tf_op jit(solution)/shard_map/ppermute | solution.py:238
  466.9 8.8 %collective-permute-done.32 = bf16[72,2560]{1,0:T(8,128)(2,1)S(1)} collective-permute-done((bf16[72,2560]{1,0:T(8,128)(2,1)S(1)}, bf16[72,2560]{1,0:T(8,128)(2,1)S(1)}, u32[]{:S(2)}, u32[]{:S(2)}) %collective-permute-start.32) | collective-permute-done | bytes 368672 | tf_op jit(solution)/shard_map/ppermute | solution.py:238
  476.2 7.9 %collective-permute-done.33 = bf16[72,2560]{1,0:T(8,128)(2,1)S(1)} collective-permute-done((bf16[72,2560]{1,0:T(8,128)(2,1)S(1)}, bf16[72,2560]{1,0:T(8,128)(2,1)S(1)}, u32[]{:S(2)}, u32[]{:S(2)}) %collective-permute-start.33) | collective-permute-done | bytes 368672 | tf_op jit(solution)/shard_map/ppermute | solution.py:238
  488.3 5.3 bitcast_convert_fusion.1
  496.3 5.2 bitcast_convert_fusion
  503.8 5.1 maximum_convert_fusion
  508.8 14.7 %reshape.360 = f32[1152,4,640]{2,1,0:T(4,128)} reshape(f32[16,72,2560]{2,1,0:T(8,128)} %maximum_convert_fusion) | data formatting | bytes 23592960 | tf_op jit(solution)/shard_map/convert_element_type | solution.py:428
  523.6 7.1 %slice.87 = f32[1152,1,576]{2,1,0:T(1,128)S(1)} slice(f32[1152,4,640]{2,1,0:T(4,128)} %reshape.360), slice={[0:1152], [3:4], [0:576]} | slice | bytes 5308416 | tf_op jit(solution)/shard_map/slice | solution.py:489
  530.6 4.6 copy.46
  535.2 13.7 %copy.47 = f32[1152,3,576]{0,2,1:T(8,128)} copy(f32[1152,3,576]{2,1,0:T(4,128)} %bitcast.224) | data formatting | bytes 15925248
  (465 shorter events, 172.8 us)
Async XLA Ops:
  6.2 11.2 %collective-permute-start = (f32[2,6912]{1,0:T(2,128)S(1)}, f32[2,6912]{1,0:T(2,128)S(1)}, u32[]{:S(2)}, u32[]{:S(2)}) collective-permute-start(f32[2,6912]{1,0:T(2,128)S(1)} %get-tuple-element.121), channel_id=1, source_target_pairs={{1,0},{0,1},{3,2},{2,3},{5,4},{4,5},{7,6},{6,7},{9,8},{8,9},{11,10... | collective-permute-start | bytes 165896 | tf_op jit(solution)/shard_map/ppermute | solution.py:166
  9.2 8.2 %collective-permute-start.2 = (f32[2,6912]{1,0:T(2,128)S(1)}, f32[2,6912]{1,0:T(2,128)S(1)}, u32[]{:S(2)}, u32[]{:S(2)}) collective-permute-start(f32[2,6912]{1,0:T(2,128)S(1)} %get-tuple-element.122), channel_id=1, source_target_pairs={{1,0},{0,1},{3,2},{2,3},{5,4},{4,5},{7,6},{6,7},{9,8},{8,9},{11,10... | collective-permute-start | bytes 165896 | tf_op jit(solution)/shard_map/ppermute | solution.py:166
  11.2 28.1 %collective-permute-start.1 = (bf16[2,192,1152]{2,1,0:T(8,128)(2,1)S(1)}, bf16[2,192,1152]{2,1,0:T(8,128)(2,1)S(1)}, u32[]{:S(2)}, u32[]{:S(2)}) collective-permute-start(bf16[2,192,1152]{2,1,0:T(8,128)(2,1)S(1)} %get-tuple-element.145), channel_id=1, source_target_pairs={{1,0},{0,1},{3,2},{2,3},{5,4},{4,5},{7,6},{6,7},{9,8},{8,9},{11,10... | collective-permute-start | bytes 2654216 | tf_op jit(solution)/shard_map/ppermute | solution.py:166
  22.7 51.4 %collective-permute-start.6 = (bf16[2,192,1152]{2,1,0:T(8,128)(2,1)S(1)}, bf16[2,192,1152]{2,1,0:T(8,128)(2,1)S(1)}, u32[]{:S(2)}, u32[]{:S(2)}) collective-permute-start(bf16[2,192,1152]{2,1,0:T(8,128)(2,1)S(1)} %get-tuple-element.150), channel_id=1, source_target_pairs={{1,0},{0,1},{3,2},{2,3},{5,4},{4,5},{7,6},{6,7},{9,8},{8,9},{11,10... | collective-permute-start | bytes 2654216 | tf_op jit(solution)/shard_map/ppermute | solution.py:166
  36.7 40.8 %collective-permute-start.4 = (bf16[384,1152]{1,0:T(8,128)(2,1)}, bf16[384,1152]{1,0:T(8,128)(2,1)}, u32[]{:S(2)}, u32[]{:S(2)}) collective-permute-start(bf16[384,1152]{1,0:T(8,128)(2,1)} %convolution_convert_fusion.12), channel_id=1, source_target_pairs={{1,0},{0,1},{3,2},{2,3},{5,4},{4,5},{7,6},{6,7},{9,8},{8,9},{11,10... | collective-permute-start | bytes 2654216 | tf_op jit(solution)/shard_map/ppermute | solution.py:166
  54.3 35.1 %collective-permute-start.3 = (bf16[384,1152]{1,0:T(8,128)(2,1)S(1)}, bf16[384,1152]{1,0:T(8,128)(2,1)}, u32[]{:S(2)}, u32[]{:S(2)}) collective-permute-start(bf16[384,1152]{1,0:T(8,128)(2,1)S(1)} %convolution_convert_fusion.11), channel_id=1, source_target_pairs={{1,0},{0,1},{3,2},{2,3},{5,4},{4,5},{7,6},{6,7},{9,8},{8,9},{11,10... | collective-permute-start | bytes 2654216 | tf_op jit(solution)/shard_map/ppermute | solution.py:166
  112.2 55.9 %collective-permute-start.5 = (bf16[384,1152]{1,0:T(8,128)(2,1)}, bf16[384,1152]{1,0:T(8,128)(2,1)}, u32[]{:S(2)}, u32[]{:S(2)}) collective-permute-start(bf16[384,1152]{1,0:T(8,128)(2,1)} %convolution_convert_fusion.9), channel_id=1, source_target_pairs={{1,0},{0,1},{3,2},{2,3},{5,4},{4,5},{7,6},{6,7},{9,8},{8,9},{11,10... | collective-permute-start | bytes 2654216 | tf_op jit(solution)/shard_map/ppermute | solution.py:166
  113.8 37.8 %collective-permute-start.7 = (bf16[384,1152]{1,0:T(8,128)(2,1)S(1)}, bf16[384,1152]{1,0:T(8,128)(2,1)S(1)}, u32[]{:S(2)}, u32[]{:S(2)}) collective-permute-start(bf16[384,1152]{1,0:T(8,128)(2,1)S(1)} %convolution_convert_fusion.6), channel_id=1, source_target_pairs={{1,0},{0,1},{3,2},{2,3},{5,4},{4,5},{7,6},{6,7},{9,8},{8,9},{11,10... | collective-permute-start | bytes 2654216 | tf_op jit(solution)/shard_map/ppermute | solution.py:166
  135.0 119.2 %collective-permute-start.51 = (bf16[8,144,1152]{2,1,0:T(8,128)(2,1)}, bf16[8,144,1152]{2,1,0:T(8,128)(2,1)}, u32[]{:S(2)}, u32[]{:S(2)}) collective-permute-start(bf16[8,144,1152]{2,1,0:T(8,128)(2,1)} %dynamic-slice_bitcast_fusion.1), channel_id=1, source_target_pairs={{0,2},{2,0},{4,6},{6,4},{8,10},{10,8},{12,14},{14,12},{16,18},{18,... | collective-permute-start | bytes 7962632 | tf_op jit(solution)/shard_map/ppermute | solution.py:241
  136.7 124.7 %collective-permute-start.35 = (bf16[8,72,2304]{2,1,0:T(8,128)(2,1)}, bf16[8,72,2304]{2,1,0:T(8,128)(2,1)}, u32[]{:S(2)}, u32[]{:S(2)}) collective-permute-start(bf16[8,72,2304]{2,1,0:T(8,128)(2,1)} %dynamic-slice_bitcast_fusion.2), channel_id=1, source_target_pairs={{0,2},{2,0},{4,6},{6,4},{8,10},{10,8},{12,14},{14,12},{16,18},{18,... | collective-permute-start | bytes 7962632 | tf_op jit(solution)/shard_map/ppermute | solution.py:241
  160.4 30.7 %collective-permute-start.8 = (bf16[384,1152]{1,0:T(8,128)(2,1)}, bf16[384,1152]{1,0:T(8,128)(2,1)}, u32[]{:S(2)}, u32[]{:S(2)}) collective-permute-start(bf16[384,1152]{1,0:T(8,128)(2,1)} %get-tuple-element.151), channel_id=1, source_target_pairs={{1,0},{0,1},{3,2},{2,3},{5,4},{4,5},{7,6},{6,7},{9,8},{8,9},{11,10... | collective-permute-start | bytes 2654216 | tf_op jit(solution)/shard_map/ppermute | solution.py:166
  222.1 19.1 %collective-permute-start.9 = (bf16[384,1152]{1,0:T(8,128)(2,1)}, bf16[384,1152]{1,0:T(8,128)(2,1)S(1)}, u32[]{:S(2)}, u32[]{:S(2)}) collective-permute-start(bf16[384,1152]{1,0:T(8,128)(2,1)} %convolution_convert_fusion.5), channel_id=1, source_target_pairs={{1,0},{0,1},{3,2},{2,3},{5,4},{4,5},{7,6},{6,7},{9,8},{8,9},{11,10... | collective-permute-start | bytes 2654216 | tf_op jit(solution)/shard_map/ppermute | solution.py:166
  231.2 159.4 %collective-permute-start.19 = (bf16[8,72,2560]{2,1,0:T(8,128)(2,1)}, bf16[8,72,2560]{2,1,0:T(8,128)(2,1)}, u32[]{:S(2)}, u32[]{:S(2)}) collective-permute-start(bf16[8,72,2560]{2,1,0:T(8,128)(2,1)} %dynamic-slice_bitcast_fusion), channel_id=1, source_target_pairs={{0,2},{2,0},{4,6},{6,4},{8,10},{10,8},{12,14},{14,12},{16,18},{18,... | collective-permute-start | bytes 8847368 | tf_op jit(solution)/shard_map/ppermute | solution.py:241
  248.0 11.7 %collective-permute-start.10 = (bf16[2,6912]{1,0:T(2,128)(2,1)S(1)}, bf16[2,6912]{1,0:T(2,128)(2,1)S(1)}, u32[]{:S(2)}, u32[]{:S(2)}) collective-permute-start(bf16[2,6912]{1,0:T(2,128)(2,1)S(1)} %constant_dynamic-update-slice_fusion), channel_id=1, source_target_pairs={{1,0},{0,1},{3,2},{2,3},{5,4},{4,5},{7,6},{6,7},{9,8},{8,9},{11,10... | collective-permute-start | bytes 82952 | tf_op jit(solution)/shard_map/ppermute | solution.py:166
  257.7 34.5 %collective-permute-start.52 = (bf16[144,1152]{1,0:T(8,128)(2,1)}, bf16[144,1152]{1,0:T(8,128)(2,1)}, u32[]{:S(2)}, u32[]{:S(2)}) collective-permute-start(bf16[144,1152]{1,0:T(8,128)(2,1)} %get-tuple-element.105), channel_id=1, source_target_pairs={{0,4},{2,6},{4,12},{6,14},{12,20},{14,22},{20,28},{22,30},{28,24},... | collective-permute-start | bytes 995336 | tf_op jit(solution)/shard_map/ppermute | solution.py:238
  259.0 36.8 %collective-permute-start.56 = (bf16[144,1152]{1,0:T(8,128)(2,1)}, bf16[144,1152]{1,0:T(8,128)(2,1)}, u32[]{:S(2)}, u32[]{:S(2)}) collective-permute-start(bf16[144,1152]{1,0:T(8,128)(2,1)} %get-tuple-element.106), channel_id=1, source_target_pairs={{0,8},{2,10},{4,0},{6,2},{12,4},{14,6},{20,12},{22,14},{28,20},{30... | collective-permute-start | bytes 995336 | tf_op jit(solution)/shard_map/ppermute | solution.py:238
  260.0 7.8 %collective-permute-start.12 = (bf16[35712]{0:T(1024)(128)(2,1)S(1)}, bf16[35712]{0:T(1024)(128)(2,1)S(1)}, u32[]{:S(2)}, u32[]{:S(2)}) collective-permute-start(bf16[35712]{0:T(1024)(128)(2,1)S(1)} %concatenate.80), channel_id=1, source_target_pairs={{0,8},{2,10},{4,0},{6,2},{12,4},{14,6},{20,12},{22,14},{28,20},{30... | collective-permute-start | bytes 214280 | tf_op jit(solution)/shard_map/ppermute | solution.py:238
  269.5 9.1 %collective-permute-start.13 = (bf16[35712]{0:T(1024)(128)(2,1)S(1)}, bf16[35712]{0:T(1024)(128)(2,1)S(1)}, u32[]{:S(2)}, u32[]{:S(2)}) collective-permute-start(bf16[35712]{0:T(1024)(128)(2,1)S(1)} %collective-permute-done.11), channel_id=1, source_target_pairs={{0,4},{2,6},{4,12},{6,14},{12,20},{14,22},{20,28},{22,30},{28,24},... | collective-permute-start | bytes 214280 | tf_op jit(solution)/shard_map/ppermute | solution.py:238
  272.2 7.8 %collective-permute-start.16 = (bf16[35712]{0:T(1024)(128)(2,1)S(1)}, bf16[35712]{0:T(1024)(128)(2,1)S(1)}, u32[]{:S(2)}, u32[]{:S(2)}) collective-permute-start(bf16[35712]{0:T(1024)(128)(2,1)S(1)} %collective-permute-done.14), channel_id=1, source_target_pairs={{0,8},{2,10},{4,0},{6,2},{12,4},{14,6},{20,12},{22,14},{28,20},{30... | collective-permute-start | bytes 214280 | tf_op jit(solution)/shard_map/ppermute | solution.py:238
  280.0 5.9 %collective-permute-start.17 = (bf16[35712]{0:T(1024)(128)(2,1)S(1)}, bf16[35712]{0:T(1024)(128)(2,1)S(1)}, u32[]{:S(2)}, u32[]{:S(2)}) collective-permute-start(bf16[35712]{0:T(1024)(128)(2,1)S(1)} %collective-permute-done.16), channel_id=1, source_target_pairs={{0,8},{2,10},{4,0},{6,2},{12,4},{14,6},{20,12},{22,14},{28,20},{30... | collective-permute-start | bytes 214280 | tf_op jit(solution)/shard_map/ppermute | solution.py:238
  283.8 9.5 %collective-permute-start.36 = (bf16[72,2304]{1,0:T(8,128)(2,1)}, bf16[72,2304]{1,0:T(8,128)(2,1)}, u32[]{:S(2)}, u32[]{:S(2)}) collective-permute-start(bf16[72,2304]{1,0:T(8,128)(2,1)} %get-tuple-element.111), channel_id=1, source_target_pairs={{8,16},{10,18},{16,24},{18,26},{24,28},{26,30},{28,20},{30,22},{20... | collective-permute-start | bytes 995336 | tf_op jit(solution)/shard_map/ppermute | solution.py:238
  285.9 21.0 %collective-permute-start.40 = (bf16[72,2304]{1,0:T(8,128)(2,1)}, bf16[72,2304]{1,0:T(8,128)(2,1)}, u32[]{:S(2)}, u32[]{:S(2)}) collective-permute-start(bf16[72,2304]{1,0:T(8,128)(2,1)} %get-tuple-element.112), channel_id=1, source_target_pairs={{8,0},{10,2},{16,8},{18,10},{24,16},{26,18},{28,24},{30,26},{20,28... | collective-permute-start | bytes 995336 | tf_op jit(solution)/shard_map/ppermute | solution.py:238
  292.2 18.9 %collective-permute-start.18 = (bf16[8,35712]{1,0:T(8,128)(2,1)}, bf16[8,35712]{1,0:T(8,128)(2,1)}, u32[]{:S(2)}, u32[]{:S(2)}) collective-permute-start(bf16[8,35712]{1,0:T(8,128)(2,1)} %stack.35), channel_id=1, source_target_pairs={{0,2},{2,0},{4,6},{6,4},{8,10},{10,8},{12,14},{14,12},{16,18},{18,... | collective-permute-start | bytes 1714184 | tf_op jit(solution)/shard_map/ppermute | solution.py:241
  293.3 10.3 %collective-permute-start.53 = (bf16[144,1152]{1,0:T(8,128)(2,1)S(1)}, bf16[144,1152]{1,0:T(8,128)(2,1)S(1)}, u32[]{:S(2)}, u32[]{:S(2)}) collective-permute-start(bf16[144,1152]{1,0:T(8,128)(2,1)S(1)} %fusion.83), channel_id=1, source_target_pairs={{0,4},{2,6},{4,12},{6,14},{12,20},{14,22},{20,28},{22,30},{28,24},... | collective-permute-start | bytes 995336 | tf_op jit(solution)/shard_map/ppermute | solution.py:238
  295.7 11.9 %collective-permute-start.37 = (bf16[72,2304]{1,0:T(8,128)(2,1)S(1)}, bf16[72,2304]{1,0:T(8,128)(2,1)S(1)}, u32[]{:S(2)}, u32[]{:S(2)}) collective-permute-start(bf16[72,2304]{1,0:T(8,128)(2,1)S(1)} %fusion.90), channel_id=1, source_target_pairs={{8,16},{10,18},{16,24},{18,26},{24,28},{26,30},{28,20},{30,22},{20... | collective-permute-start | bytes 995336 | tf_op jit(solution)/shard_map/ppermute | solution.py:238
  305.6 32.4 %collective-permute-start.54 = (bf16[144,1152]{1,0:T(8,128)(2,1)}, bf16[144,1152]{1,0:T(8,128)(2,1)}, u32[]{:S(2)}, u32[]{:S(2)}) collective-permute-start(bf16[144,1152]{1,0:T(8,128)(2,1)} %get-tuple-element.103), channel_id=1, source_target_pairs={{0,4},{2,6},{4,12},{6,14},{12,20},{14,22},{20,28},{22,30},{28,24},... | collective-permute-start | bytes 995336 | tf_op jit(solution)/shard_map/ppermute | solution.py:238
  306.8 31.2 %collective-permute-start.57 = (bf16[144,1152]{1,0:T(8,128)(2,1)}, bf16[144,1152]{1,0:T(8,128)(2,1)}, u32[]{:S(2)}, u32[]{:S(2)}) collective-permute-start(bf16[144,1152]{1,0:T(8,128)(2,1)} %get-tuple-element.104), channel_id=1, source_target_pairs={{0,8},{2,10},{4,0},{6,2},{12,4},{14,6},{20,12},{22,14},{28,20},{30... | collective-permute-start | bytes 995336 | tf_op jit(solution)/shard_map/ppermute | solution.py:238
  309.7 31.6 %collective-permute-start.38 = (bf16[72,2304]{1,0:T(8,128)(2,1)}, bf16[72,2304]{1,0:T(8,128)(2,1)}, u32[]{:S(2)}, u32[]{:S(2)}) collective-permute-start(bf16[72,2304]{1,0:T(8,128)(2,1)} %get-tuple-element.109), channel_id=1, source_target_pairs={{8,16},{10,18},{16,24},{18,26},{24,28},{26,30},{28,20},{30,22},{20... | collective-permute-start | bytes 995336 | tf_op jit(solution)/shard_map/ppermute | solution.py:238
  311.1 30.3 %collective-permute-start.41 = (bf16[72,2304]{1,0:T(8,128)(2,1)}, bf16[72,2304]{1,0:T(8,128)(2,1)}, u32[]{:S(2)}, u32[]{:S(2)}) collective-permute-start(bf16[72,2304]{1,0:T(8,128)(2,1)} %get-tuple-element.110), channel_id=1, source_target_pairs={{8,0},{10,2},{16,8},{18,10},{24,16},{26,18},{28,24},{30,26},{20,28... | collective-permute-start | bytes 995336 | tf_op jit(solution)/shard_map/ppermute | solution.py:238
  339.3 10.7 %collective-permute-start.55 = (bf16[144,1152]{1,0:T(8,128)(2,1)S(1)}, bf16[144,1152]{1,0:T(8,128)(2,1)S(1)}, u32[]{:S(2)}, u32[]{:S(2)}) collective-permute-start(bf16[144,1152]{1,0:T(8,128)(2,1)S(1)} %get-tuple-element.101), channel_id=1, source_target_pairs={{0,4},{2,6},{4,12},{6,14},{12,20},{14,22},{20,28},{22,30},{28,24},... | collective-permute-start | bytes 995336 | tf_op jit(solution)/shard_map/ppermute | solution.py:238
  340.6 10.7 %collective-permute-start.58 = (bf16[144,1152]{1,0:T(8,128)(2,1)S(1)}, bf16[144,1152]{1,0:T(8,128)(2,1)S(1)}, u32[]{:S(2)}, u32[]{:S(2)}) collective-permute-start(bf16[144,1152]{1,0:T(8,128)(2,1)S(1)} %get-tuple-element.102), channel_id=1, source_target_pairs={{0,8},{2,10},{4,0},{6,2},{12,4},{14,6},{20,12},{22,14},{28,20},{30... | collective-permute-start | bytes 995336 | tf_op jit(solution)/shard_map/ppermute | solution.py:238
  342.8 15.6 %collective-permute-start.39 = (bf16[72,2304]{1,0:T(8,128)(2,1)S(1)}, bf16[72,2304]{1,0:T(8,128)(2,1)S(1)}, u32[]{:S(2)}, u32[]{:S(2)}) collective-permute-start(bf16[72,2304]{1,0:T(8,128)(2,1)S(1)} %get-tuple-element.107), channel_id=1, source_target_pairs={{8,16},{10,18},{16,24},{18,26},{24,28},{26,30},{28,20},{30,22},{20... | collective-permute-start | bytes 995336 | tf_op jit(solution)/shard_map/ppermute | solution.py:238
  344.1 14.2 %collective-permute-start.42 = (bf16[72,2304]{1,0:T(8,128)(2,1)S(1)}, bf16[72,2304]{1,0:T(8,128)(2,1)S(1)}, u32[]{:S(2)}, u32[]{:S(2)}) collective-permute-start(bf16[72,2304]{1,0:T(8,128)(2,1)S(1)} %get-tuple-element.108), channel_id=1, source_target_pairs={{8,0},{10,2},{16,8},{18,10},{24,16},{26,18},{28,24},{30,26},{20,28... | collective-permute-start | bytes 995336 | tf_op jit(solution)/shard_map/ppermute | solution.py:238
  352.3 12.1 %collective-permute-start.59 = (bf16[144,1152]{1,0:T(8,128)(2,1)}, bf16[144,1152]{1,0:T(8,128)(2,1)}, u32[]{:S(2)}, u32[]{:S(2)}) collective-permute-start(bf16[144,1152]{1,0:T(8,128)(2,1)} %get-tuple-element.69), channel_id=1, source_target_pairs={{0,4},{2,6},{4,12},{6,14},{12,20},{14,22},{20,28},{22,30},{28,24},... | collective-permute-start | bytes 995336 | tf_op jit(solution)/shard_map/ppermute | solution.py:238
  353.9 12.1 %collective-permute-start.60 = (bf16[144,1152]{1,0:T(8,128)(2,1)}, bf16[144,1152]{1,0:T(8,128)(2,1)}, u32[]{:S(2)}, u32[]{:S(2)}) collective-permute-start(bf16[144,1152]{1,0:T(8,128)(2,1)} %get-tuple-element.69), channel_id=1, source_target_pairs={{0,8},{2,10},{4,0},{6,2},{12,4},{14,6},{20,12},{22,14},{28,20},{30... | collective-permute-start | bytes 995336 | tf_op jit(solution)/shard_map/ppermute | solution.py:238
  360.4 12.3 %collective-permute-start.43 = (bf16[72,2304]{1,0:T(8,128)(2,1)}, bf16[72,2304]{1,0:T(8,128)(2,1)}, u32[]{:S(2)}, u32[]{:S(2)}) collective-permute-start(bf16[72,2304]{1,0:T(8,128)(2,1)} %get-tuple-element.71), channel_id=1, source_target_pairs={{8,16},{10,18},{16,24},{18,26},{24,28},{26,30},{28,20},{30,22},{20... | collective-permute-start | bytes 995336 | tf_op jit(solution)/shard_map/ppermute | solution.py:238
  363.2 11.3 %collective-permute-start.44 = (bf16[72,2304]{1,0:T(8,128)(2,1)}, bf16[72,2304]{1,0:T(8,128)(2,1)S(1)}, u32[]{:S(2)}, u32[]{:S(2)}) collective-permute-start(bf16[72,2304]{1,0:T(8,128)(2,1)} %get-tuple-element.71), channel_id=1, source_target_pairs={{8,0},{10,2},{16,8},{18,10},{24,16},{26,18},{28,24},{30,26},{20,28... | collective-permute-start | bytes 995336 | tf_op jit(solution)/shard_map/ppermute | solution.py:238
  364.4 16.0 %collective-permute-start.61 = (bf16[144,1152]{1,0:T(8,128)(2,1)}, bf16[144,1152]{1,0:T(8,128)(2,1)S(1)}, u32[]{:S(2)}, u32[]{:S(2)}) collective-permute-start(bf16[144,1152]{1,0:T(8,128)(2,1)} %collective-permute-done.59), channel_id=1, source_target_pairs={{0,4},{2,6},{4,12},{6,14},{12,20},{14,22},{20,28},{22,30},{28,24},... | collective-permute-start | bytes 995336 | tf_op jit(solution)/shard_map/ppermute | solution.py:238
  366.0 15.6 %collective-permute-start.62 = (bf16[144,1152]{1,0:T(8,128)(2,1)}, bf16[144,1152]{1,0:T(8,128)(2,1)S(1)}, u32[]{:S(2)}, u32[]{:S(2)}) collective-permute-start(bf16[144,1152]{1,0:T(8,128)(2,1)} %collective-permute-done.60), channel_id=1, source_target_pairs={{0,8},{2,10},{4,0},{6,2},{12,4},{14,6},{20,12},{22,14},{28,20},{30... | collective-permute-start | bytes 995336 | tf_op jit(solution)/shard_map/ppermute | solution.py:238
  372.7 14.1 %collective-permute-start.45 = (bf16[72,2304]{1,0:T(8,128)(2,1)}, bf16[72,2304]{1,0:T(8,128)(2,1)S(1)}, u32[]{:S(2)}, u32[]{:S(2)}) collective-permute-start(bf16[72,2304]{1,0:T(8,128)(2,1)} %collective-permute-done.43), channel_id=1, source_target_pairs={{8,16},{10,18},{16,24},{18,26},{24,28},{26,30},{28,20},{30,22},{20... | collective-permute-start | bytes 995336 | tf_op jit(solution)/shard_map/ppermute | solution.py:238
  374.5 13.1 %collective-permute-start.46 = (bf16[72,2304]{1,0:T(8,128)(2,1)S(1)}, bf16[72,2304]{1,0:T(8,128)(2,1)S(1)}, u32[]{:S(2)}, u32[]{:S(2)}) collective-permute-start(bf16[72,2304]{1,0:T(8,128)(2,1)S(1)} %collective-permute-done.44), channel_id=1, source_target_pairs={{8,0},{10,2},{16,8},{18,10},{24,16},{26,18},{28,24},{30,26},{20,28... | collective-permute-start | bytes 995336 | tf_op jit(solution)/shard_map/ppermute | solution.py:238
  380.4 30.6 %collective-permute-start.63 = (bf16[144,1152]{1,0:T(8,128)(2,1)S(1)}, bf16[144,1152]{1,0:T(8,128)(2,1)S(1)}, u32[]{:S(2)}, u32[]{:S(2)}) collective-permute-start(bf16[144,1152]{1,0:T(8,128)(2,1)S(1)} %collective-permute-done.61), channel_id=1, source_target_pairs={{0,4},{2,6},{4,12},{6,14},{12,20},{14,22},{20,28},{22,30},{28,24},... | collective-permute-start | bytes 995336 | tf_op jit(solution)/shard_map/ppermute | solution.py:238
  381.7 14.2 %collective-permute-start.64 = (bf16[144,1152]{1,0:T(8,128)(2,1)S(1)}, bf16[144,1152]{1,0:T(8,128)(2,1)S(1)}, u32[]{:S(2)}, u32[]{:S(2)}) collective-permute-start(bf16[144,1152]{1,0:T(8,128)(2,1)S(1)} %collective-permute-done.62), channel_id=1, source_target_pairs={{0,8},{2,10},{4,0},{6,2},{12,4},{14,6},{20,12},{22,14},{28,20},{30... | collective-permute-start | bytes 995336 | tf_op jit(solution)/shard_map/ppermute | solution.py:238
  386.8 14.2 %collective-permute-start.47 = (bf16[72,2304]{1,0:T(8,128)(2,1)S(1)}, bf16[72,2304]{1,0:T(8,128)(2,1)S(1)}, u32[]{:S(2)}, u32[]{:S(2)}) collective-permute-start(bf16[72,2304]{1,0:T(8,128)(2,1)S(1)} %collective-permute-done.45), channel_id=1, source_target_pairs={{8,16},{10,18},{16,24},{18,26},{24,28},{26,30},{28,20},{30,22},{20... | collective-permute-start | bytes 995336 | tf_op jit(solution)/shard_map/ppermute | solution.py:238
  387.6 14.2 %collective-permute-start.48 = (bf16[72,2304]{1,0:T(8,128)(2,1)S(1)}, bf16[72,2304]{1,0:T(8,128)(2,1)S(1)}, u32[]{:S(2)}, u32[]{:S(2)}) collective-permute-start(bf16[72,2304]{1,0:T(8,128)(2,1)S(1)} %collective-permute-done.46), channel_id=1, source_target_pairs={{8,0},{10,2},{16,8},{18,10},{24,16},{26,18},{28,24},{30,26},{20,28... | collective-permute-start | bytes 995336 | tf_op jit(solution)/shard_map/ppermute | solution.py:238
  394.2 15.5 %collective-permute-start.20 = (bf16[72,2560]{1,0:T(8,128)(2,1)S(1)}, bf16[72,2560]{1,0:T(8,128)(2,1)S(1)}, u32[]{:S(2)}, u32[]{:S(2)}) collective-permute-start(bf16[72,2560]{1,0:T(8,128)(2,1)S(1)} %get-tuple-element.99), channel_id=1, source_target_pairs={{0,4},{2,6},{4,12},{6,14},{12,20},{14,22},{20,28},{22,30},{28,24},... | collective-permute-start | bytes 1105928 | tf_op jit(solution)/shard_map/ppermute | solution.py:238
  395.8 15.3 %collective-permute-start.24 = (bf16[72,2560]{1,0:T(8,128)(2,1)S(1)}, bf16[72,2560]{1,0:T(8,128)(2,1)S(1)}, u32[]{:S(2)}, u32[]{:S(2)}) collective-permute-start(bf16[72,2560]{1,0:T(8,128)(2,1)S(1)} %get-tuple-element.100), channel_id=1, source_target_pairs={{0,8},{2,10},{4,0},{6,2},{12,4},{14,6},{20,12},{22,14},{28,20},{30... | collective-permute-start | bytes 1105928 | tf_op jit(solution)/shard_map/ppermute | solution.py:238
  401.0 34.9 %collective-permute-start.65 = (bf16[144,1152]{1,0:T(8,128)(2,1)S(1)}, bf16[144,1152]{1,0:T(8,128)(2,1)S(1)}, u32[]{:S(2)}, u32[]{:S(2)}) collective-permute-start(bf16[144,1152]{1,0:T(8,128)(2,1)S(1)} %collective-permute-done.64), channel_id=1, source_target_pairs={{0,8},{2,10},{4,0},{6,2},{12,4},{14,6},{20,12},{22,14},{28,20},{30... | collective-permute-start | bytes 995336 | tf_op jit(solution)/shard_map/ppermute | solution.py:238
  401.8 43.5 %collective-permute-start.49 = (bf16[72,2304]{1,0:T(8,128)(2,1)S(1)}, bf16[72,2304]{1,0:T(8,128)(2,1)S(1)}, u32[]{:S(2)}, u32[]{:S(2)}) collective-permute-start(bf16[72,2304]{1,0:T(8,128)(2,1)S(1)} %collective-permute-done.48), channel_id=1, source_target_pairs={{8,0},{10,2},{16,8},{18,10},{24,16},{26,18},{28,24},{30,26},{20,28... | collective-permute-start | bytes 995336 | tf_op jit(solution)/shard_map/ppermute | solution.py:238
  409.8 11.9 %collective-permute-start.21 = (bf16[72,2560]{1,0:T(8,128)(2,1)S(1)}, bf16[72,2560]{1,0:T(8,128)(2,1)S(1)}, u32[]{:S(2)}, u32[]{:S(2)}) collective-permute-start(bf16[72,2560]{1,0:T(8,128)(2,1)S(1)} %fusion.76), channel_id=1, source_target_pairs={{0,4},{2,6},{4,12},{6,14},{12,20},{14,22},{20,28},{22,30},{28,24},... | collective-permute-start | bytes 1105928 | tf_op jit(solution)/shard_map/ppermute | solution.py:238
  421.9 10.2 %collective-permute-start.22 = (bf16[72,2560]{1,0:T(8,128)(2,1)S(1)}, bf16[72,2560]{1,0:T(8,128)(2,1)S(1)}, u32[]{:S(2)}, u32[]{:S(2)}) collective-permute-start(bf16[72,2560]{1,0:T(8,128)(2,1)S(1)} %get-tuple-element.97), channel_id=1, source_target_pairs={{0,4},{2,6},{4,12},{6,14},{12,20},{14,22},{20,28},{22,30},{28,24},... | collective-permute-start | bytes 1105928 | tf_op jit(solution)/shard_map/ppermute | solution.py:238
  423.2 10.4 %collective-permute-start.25 = (bf16[72,2560]{1,0:T(8,128)(2,1)S(1)}, bf16[72,2560]{1,0:T(8,128)(2,1)S(1)}, u32[]{:S(2)}, u32[]{:S(2)}) collective-permute-start(bf16[72,2560]{1,0:T(8,128)(2,1)S(1)} %get-tuple-element.98), channel_id=1, source_target_pairs={{0,8},{2,10},{4,0},{6,2},{12,4},{14,6},{20,12},{22,14},{28,20},{30... | collective-permute-start | bytes 1105928 | tf_op jit(solution)/shard_map/ppermute | solution.py:238
  433.9 9.4 %collective-permute-start.23 = (bf16[72,2560]{1,0:T(8,128)(2,1)S(1)}, bf16[72,2560]{1,0:T(8,128)(2,1)S(1)}, u32[]{:S(2)}, u32[]{:S(2)}) collective-permute-start(bf16[72,2560]{1,0:T(8,128)(2,1)S(1)} %get-tuple-element.95), channel_id=1, source_target_pairs={{0,4},{2,6},{4,12},{6,14},{12,20},{14,22},{20,28},{22,30},{28,24},... | collective-permute-start | bytes 1105928 | tf_op jit(solution)/shard_map/ppermute | solution.py:238
  435.5 7.8 %collective-permute-start.26 = (bf16[72,2560]{1,0:T(8,128)(2,1)S(1)}, bf16[72,2560]{1,0:T(8,128)(2,1)S(1)}, u32[]{:S(2)}, u32[]{:S(2)}) collective-permute-start(bf16[72,2560]{1,0:T(8,128)(2,1)S(1)} %get-tuple-element.96), channel_id=1, source_target_pairs={{0,8},{2,10},{4,0},{6,2},{12,4},{14,6},{20,12},{22,14},{28,20},{30... | collective-permute-start | bytes 1105928 | tf_op jit(solution)/shard_map/ppermute | solution.py:238
  436.0 57.6 %collective-permute-start.66 = (bf16[8,144,1152]{2,1,0:T(8,128)(2,1)S(1)}, bf16[8,144,1152]{2,1,0:T(8,128)(2,1)}, u32[]{:S(2)}, u32[]{:S(2)}) collective-permute-start(bf16[8,144,1152]{2,1,0:T(8,128)(2,1)S(1)} %bitcast_dynamic-update-slice_fusion.8), channel_id=1, source_target_pairs={{0,2},{2,0},{4,6},{6,4},{8,10},{10,8},{12,14},{14,12},{16,18},{18,... | collective-permute-start | bytes 7962632 | tf_op jit(solution)/shard_map/ppermute | solution.py:241
  443.6 10.1 %collective-permute-start.27 = (bf16[72,2560]{1,0:T(8,128)(2,1)S(1)}, bf16[72,2560]{1,0:T(8,128)(2,1)S(1)}, u32[]{:S(2)}, u32[]{:S(2)}) collective-permute-start(bf16[72,2560]{1,0:T(8,128)(2,1)S(1)} %get-tuple-element.73), channel_id=1, source_target_pairs={{0,4},{2,6},{4,12},{6,14},{12,20},{14,22},{20,28},{22,30},{28,24},... | collective-permute-start | bytes 1105928 | tf_op jit(solution)/shard_map/ppermute | solution.py:238
  445.3 38.9 %collective-permute-start.50 = (bf16[8,72,2304]{2,1,0:T(8,128)(2,1)S(1)}, bf16[8,72,2304]{2,1,0:T(8,128)(2,1)S(1)}, u32[]{:S(2)}, u32[]{:S(2)}) collective-permute-start(bf16[8,72,2304]{2,1,0:T(8,128)(2,1)S(1)} %bitcast_dynamic-update-slice_fusion.16), channel_id=1, source_target_pairs={{0,2},{2,0},{4,6},{6,4},{8,10},{10,8},{12,14},{14,12},{16,18},{18,... | collective-permute-start | bytes 7962632 | tf_op jit(solution)/shard_map/ppermute | solution.py:241
  445.4 11.0 %collective-permute-start.28 = (bf16[72,2560]{1,0:T(8,128)(2,1)S(1)}, bf16[72,2560]{1,0:T(8,128)(2,1)S(1)}, u32[]{:S(2)}, u32[]{:S(2)}) collective-permute-start(bf16[72,2560]{1,0:T(8,128)(2,1)S(1)} %get-tuple-element.73), channel_id=1, source_target_pairs={{0,8},{2,10},{4,0},{6,2},{12,4},{14,6},{20,12},{22,14},{28,20},{30... | collective-permute-start | bytes 1105928 | tf_op jit(solution)/shard_map/ppermute | solution.py:238
  453.8 10.0 %collective-permute-start.29 = (bf16[72,2560]{1,0:T(8,128)(2,1)S(1)}, bf16[72,2560]{1,0:T(8,128)(2,1)S(1)}, u32[]{:S(2)}, u32[]{:S(2)}) collective-permute-start(bf16[72,2560]{1,0:T(8,128)(2,1)S(1)} %collective-permute-done.27), channel_id=1, source_target_pairs={{0,4},{2,6},{4,12},{6,14},{12,20},{14,22},{20,28},{22,30},{28,24},... | collective-permute-start | bytes 1105928 | tf_op jit(solution)/shard_map/ppermute | solution.py:238
  456.4 10.1 %collective-permute-start.30 = (bf16[72,2560]{1,0:T(8,128)(2,1)S(1)}, bf16[72,2560]{1,0:T(8,128)(2,1)S(1)}, u32[]{:S(2)}, u32[]{:S(2)}) collective-permute-start(bf16[72,2560]{1,0:T(8,128)(2,1)S(1)} %collective-permute-done.28), channel_id=1, source_target_pairs={{0,8},{2,10},{4,0},{6,2},{12,4},{14,6},{20,12},{22,14},{28,20},{30... | collective-permute-start | bytes 1105928 | tf_op jit(solution)/shard_map/ppermute | solution.py:238
  463.7 12.4 %collective-permute-start.31 = (bf16[72,2560]{1,0:T(8,128)(2,1)S(1)}, bf16[72,2560]{1,0:T(8,128)(2,1)S(1)}, u32[]{:S(2)}, u32[]{:S(2)}) collective-permute-start(bf16[72,2560]{1,0:T(8,128)(2,1)S(1)} %collective-permute-done.29), channel_id=1, source_target_pairs={{0,4},{2,6},{4,12},{6,14},{12,20},{14,22},{20,28},{22,30},{28,24},... | collective-permute-start | bytes 1105928 | tf_op jit(solution)/shard_map/ppermute | solution.py:238
  466.5 9.2 %collective-permute-start.32 = (bf16[72,2560]{1,0:T(8,128)(2,1)S(1)}, bf16[72,2560]{1,0:T(8,128)(2,1)S(1)}, u32[]{:S(2)}, u32[]{:S(2)}) collective-permute-start(bf16[72,2560]{1,0:T(8,128)(2,1)S(1)} %collective-permute-done.30), channel_id=1, source_target_pairs={{0,8},{2,10},{4,0},{6,2},{12,4},{14,6},{20,12},{22,14},{28,20},{30... | collective-permute-start | bytes 1105928 | tf_op jit(solution)/shard_map/ppermute | solution.py:238
  475.7 8.4 %collective-permute-start.33 = (bf16[72,2560]{1,0:T(8,128)(2,1)S(1)}, bf16[72,2560]{1,0:T(8,128)(2,1)S(1)}, u32[]{:S(2)}, u32[]{:S(2)}) collective-permute-start(bf16[72,2560]{1,0:T(8,128)(2,1)S(1)} %collective-permute-done.32), channel_id=1, source_target_pairs={{0,8},{2,10},{4,0},{6,2},{12,4},{14,6},{20,12},{22,14},{28,20},{30... | collective-permute-start | bytes 1105928 | tf_op jit(solution)/shard_map/ppermute | solution.py:238
  484.1 17.4 %collective-permute-start.34 = (bf16[8,72,2560]{2,1,0:T(8,128)(2,1)S(1)}, bf16[8,72,2560]{2,1,0:T(8,128)(2,1)}, u32[]{:S(2)}, u32[]{:S(2)}) collective-permute-start(bf16[8,72,2560]{2,1,0:T(8,128)(2,1)S(1)} %bitcast_dynamic-update-slice_fusion), channel_id=1, source_target_pairs={{0,2},{2,0},{4,6},{6,4},{8,10},{10,8},{12,14},{14,12},{16,18},{18,... | collective-permute-start | bytes 8847368 | tf_op jit(solution)/shard_map/ppermute | solution.py:241
  (105 other events, 506.6 us)
